TPU v7x, 32 devices: a whole 2x2x4 slice. The times are simulated.
32 devices in a mesh: wide: 16 (over z, y, x), clus: 2 (over core).
Axes of the slice: x: 2, y: 2, z: 4, core: 2. Of those that a mesh axis runs over, the one named last changes fastest.
Arguments:
- duals: bfloat16 [96, 64, 3840], P(None, ('wide', 'clus')), may hold values from -6 to 6
- kernel: bfloat16 [64, 6, 3840], P(('wide', 'clus')), may hold values from -0.29882812 to 0.29882812
- sub_counts: int32 [32], P(('wide', 'clus')), may hold values from 1 to 2, as said below
- dual_sizes: int32 [64], P(('wide', 'clus')), may hold values from 1920 to 3840, as said below
- cluster_factor: float32 [16, 24, 24], P('wide'), as said below
- coarse_map: int32 [16, 24], P('wide'), may hold values from 0 to 383, as said below
- coarse_inverse: float32 [384, 384], P(None, 'clus'), as said below
Outputs:
- projected: bfloat16 [96, 64, 3840], P(None, ('wide', 'clus'))
Inputs may be any that keep to these rules, and one draw needn't show every extreme that they name: `sub_counts`: each device holds 1 to 2 subdomains; some device holds 2. `dual_sizes`: some slot has the full 3840. `coarse_map`: the rows of cluster w map into the 48 global rows that begin at w * 24, counted modulo 384. `cluster_factor`: lower triangular with diagonal entries between 1 and 2. `coarse_inverse`: diagonal entries between 1 and 2.
All inputs are finite; a program needn't handle non-finite values.
Results may differ from a plain program's by a relative error of at most 0.0018.
Values sent between devices are 32-bit elements; how exact they have to be, the bound alone decides.
No kernel may reach another device: no remote copies, remote signals or barrier semaphores. Data moves between devices by JAX's collectives and lax.ppermute only.
A program may use at most 64 MiB of HBM per device.

v0:
```python
import jax
import jax.numpy as jnp
from jax import lax
from jax.sharding import PartitionSpec as P


def per_device(duals, kernel, sub_counts, dual_sizes, cluster_factor, coarse_map, coarse_inverse):
    rhs_count, sub_count, dual_width = duals.shape
    mode_count = kernel.shape[1]
    hi = lax.Precision.HIGHEST
    position = lax.broadcasted_iota(jnp.int32, (sub_count, dual_width), 1)
    slot_index = lax.broadcasted_iota(jnp.int32, (sub_count, dual_width), 0)
    active = (position < dual_sizes[:, None]) & (slot_index < sub_counts[0])
    masked = jnp.where(active[:, None, :], kernel, jnp.zeros_like(kernel))
    local = jnp.einsum("rsi,ski->rsk", duals, masked, preferred_element_type=jnp.float32)
    local = local.reshape(rhs_count, sub_count * mode_count)
    cluster_vec = lax.all_gather(local, "clus", axis=1, tiled=True)
    lower = cluster_factor[0]
    rows_map = coarse_map[0]
    cluster_rows = rows_map.shape[0]
    global_rows = coarse_inverse.shape[0]
    forward = lax.linalg.triangular_solve(lower, cluster_vec.T, left_side=True, lower=True).T
    one_hot = (
        rows_map[:, None] == lax.broadcasted_iota(jnp.int32, (cluster_rows, global_rows), 1)
    ).astype(jnp.float32)
    part_sum = jnp.dot(forward, one_hot, precision=hi)
    gsum = lax.psum(part_sum, "wide")
    beta_part = jnp.dot(gsum, coarse_inverse, precision=hi)
    beta = lax.all_gather(beta_part, "clus", axis=1, tiled=True)
    back = jnp.dot(beta, one_hot.T, precision=hi)
    corr = lax.linalg.triangular_solve(
        lower, (forward - back).T, left_side=True, lower=True, transpose_a=True
    )
    own_rows = lax.dynamic_slice_in_dim(
        corr, lax.axis_index("clus") * sub_count * mode_count, sub_count * mode_count, 0
    )
    own_corr = own_rows.T.reshape(rhs_count, sub_count, mode_count).astype(jnp.bfloat16)
    delta = jnp.einsum("rsk,ski->rsi", own_corr, masked, preferred_element_type=jnp.float32)
    return (duals.astype(jnp.float32) - delta).astype(jnp.bfloat16)


def solution(mesh):
    in_specs = (
        P(None, ("wide", "clus"), None),
        P(("wide", "clus"), None, None),
        P(("wide", "clus")),
        P(("wide", "clus")),
        P("wide", None, None),
        P("wide", None),
        P(None, "clus"),
    )
    out_specs = P(None, ("wide", "clus"), None)
    return jax.shard_map(
        per_device, mesh=mesh, in_specs=in_specs, out_specs=out_specs, check_vma=False
    )
```

profile of v0, /device:TPU:0, one launch (start us, length us, event | category | flops | bytes accessed | tf_op | source)
XLA Modules:
  0.0 140.0 jit_solution(6165059862386261918)
XLA Ops:
  6.5 0.0 copy-start
  6.5 0.0 copy-start.2
  6.5 0.0 all-reduce.2.cloned.1.call-start
  7.3 0.7 fusion.16
  8.0 1.8 %custom-call.5 = f32[1,24,24]{1,2,0:T(8,128)S(1)} custom-call(f32[1,24,24]{2,1,0:T(8,128)S(1)} %fusion.16), custom_call_target="InvertDiagBlocksLowerTriangular" | custom-call | tf_op jit(solution)/shard_map/triangular_solve | solution.py:31
  9.8 0.8 compare_and_fusion
  10.6 1.0 broadcast_select_fusion
  11.6 0.0 copy-start.1
  11.6 2.0 %fusion.4 = f32[96,2,6]{0,2,1:T(8,128)S(1)} fusion(bf16[96,2,3840]{2,1,0:T(2,128)(2,1)} %param.7, bf16[2,6,3840]{2,0,1:T(2,128)(2,1)S(1)} %broadcast_select_fusion), kind=kOutput, calls=%fused_computation.6 | convolution fusion | flops 8847360 | bytes 1571328 | tf_op jit(solution)/shard_map/rsi,ski->rsk/dot_general | solution.py:15
  13.5 2.0 %all-gather = f32[2,12,96]{2,1,0:T(8,128)S(1)} all-gather(f32[1,12,96]{2,1,0:T(8,128)S(1)} %bitcast.34), channel_id=1, replica_groups=mesh['wide'=16,'clus'=2] {'clus'}, dimensions={0}, use_global_device_ids=true | all-gather | bytes 13824 | tf_op jit(solution)/shard_map/all_gather | solution.py:17
  15.5 0.2 fusion.14
  15.7 0.0 copy-done.2
  15.7 0.9 fusion.9
  16.7 0.0 all-reduce.2.cloned.1.call-update
  16.7 109.5 %all-reduce.2.cloned.1.call-done = f32[96,384]{1,0:T(8,128)} async-done(((f32[96,384]{1,0:T(8,128)}), f32[96,384]{1,0:T(8,128)}) %all-reduce.2.cloned.1.call-update) | async-done | bytes 147472 | tf_op jit(solution)/shard_map/psum | solution.py:27
  126.2 0.0 copy-done
  126.2 1.3 fusion.18
  127.5 1.9 %all_gather.7 = f32[96,384]{0,1:T(8,128)S(1)} all-gather(f32[96,192]{0,1:T(8,128)S(1)} %fusion.18), channel_id=1, replica_groups=mesh['wide'=16,'clus'=2] {'clus'}, dimensions={1}, use_global_device_ids=true | all-gather | bytes 221184 | tf_op jit(solution)/shard_map/all_gather | solution.py:29
  129.5 0.2 convolution_subtract_fusion
  129.7 0.1 fusion.12
  129.9 0.0 copy-done.1
  129.9 0.6 fusion.1
  130.5 2.6 %copy.23 = bf16[96,2,3840]{2,1,0:T(2,128)(2,1)} copy(bf16[96,2,3840]{2,0,1:T(8,128)(2,1)S(1)} %fusion.1) | data formatting | bytes 2949120 | tf_op jit(solution)/shard_map/convert_element_type | solution.py:39
  (5 shorter events, 0.1 us)
Async XLA Ops:
  6.5 119.7 %copy-start = (f32[384,192]{0,1:T(8,128)S(1)}, f32[384,192]{0,1:T(8,128)}, u32[]{:S(2)}) copy-start(f32[384,192]{0,1:T(8,128)} %param.13) | copy-start | bytes 884740
  6.5 9.2 %copy-start.2 = (s32[1,24]{1,0:T(1,128)S(1)}, s32[1,24]{1,0:T(1,128)}, u32[]{:S(2)}) copy-start(s32[1,24]{1,0:T(1,128)} %param.12) | copy-start | bytes 292
  6.5 119.7 %all-reduce.2.cloned.1.call-start = ((), (), s32[]{:S(2)}) async-start(), calls=%async_computation | async-start | bytes 294912 | tf_op jit(solution)/shard_map/psum | solution.py:27
  11.6 118.3 %copy-start.1 = (bf16[96,2,3840]{2,1,0:T(2,128)(2,1)S(1)}, bf16[96,2,3840]{2,1,0:T(2,128)(2,1)}, u32[]{:S(2)}) copy-start(bf16[96,2,3840]{2,1,0:T(2,128)(2,1)} %param.7) | copy-start | bytes 4423684
Sparse Core Ops, SparseCore 0:
  16.8 109.3 all-reduce.1
where the time goes:
time: 140 us
  waiting for transfers between devices  110 us (79%)
  between operations  14.2 us (10%)
  matrix products  5.34 us (4%)
  other arithmetic  4.31 us (3%)
  blocking collectives  3.92 us (3%)
  local copies, waits for them, and re-layouts  2.7 us (2%)
    psum x1, waiting for transfers between devices, per_device(): gsum = lax.psum(part_sum, 'wide')  110 us
  transfers between devices with their start and end apart: 1, of which 1 were waited for; matrix products, arithmetic and copies ran while one was open for 0% of the time, Pallas kernels for 0%

commit v1 on v0

--- a/solution.py
+++ b/solution.py
@@ -19,17 +19,25 @@
     rows_map = coarse_map[0]
     cluster_rows = rows_map.shape[0]
     global_rows = coarse_inverse.shape[0]
-    forward = lax.linalg.triangular_solve(lower, cluster_vec.T, left_side=True, lower=True).T
+    clusters = lax.axis_size("wide")
+    forward = lax.linalg.triangular_solve(lower, cluster_vec.T, left_side=True, lower=True)
+    payload = jnp.concatenate([forward, rows_map.astype(jnp.float32)[:, None]], axis=1)
+    spread = jnp.broadcast_to(payload[None], (clusters,) + payload.shape)
+    gathered = lax.all_to_all(spread, "wide", 0, 0).reshape(clusters * cluster_rows, rhs_count + 1)
+    all_forward = gathered[:, :rhs_count]
+    all_map = gathered[:, rhs_count].astype(jnp.int32)
+    all_hot = (
+        all_map[:, None] == lax.broadcasted_iota(jnp.int32, (clusters * cluster_rows, global_rows), 1)
+    ).astype(jnp.float32)
+    gsum = lax.dot_general(all_forward, all_hot, (((0,), (0,)), ((), ())), precision=hi)
+    beta_part = jnp.dot(gsum, coarse_inverse, precision=hi)
+    beta = lax.all_gather(beta_part, "clus", axis=1, tiled=True)
     one_hot = (
         rows_map[:, None] == lax.broadcasted_iota(jnp.int32, (cluster_rows, global_rows), 1)
     ).astype(jnp.float32)
-    part_sum = jnp.dot(forward, one_hot, precision=hi)
-    gsum = lax.psum(part_sum, "wide")
-    beta_part = jnp.dot(gsum, coarse_inverse, precision=hi)
-    beta = lax.all_gather(beta_part, "clus", axis=1, tiled=True)
-    back = jnp.dot(beta, one_hot.T, precision=hi)
+    back = jnp.dot(one_hot, beta.T, precision=hi)
     corr = lax.linalg.triangular_solve(
-        lower, (forward - back).T, left_side=True, lower=True, transpose_a=True
+        lower, forward - back, left_side=True, lower=True, transpose_a=True
     )
     own_rows = lax.dynamic_slice_in_dim(
         corr, lax.axis_index("clus") * sub_count * mode_count, sub_count * mode_count, 0

time: 140 us -> 35 us (0.25)
  waiting for transfers between devices: 110 us -> 8.96 us
  between operations: 14.2 us -> 0.79 us
  starting transfers between devices: 0.01 us -> 8.19 us
  matrix products: 5.34 us -> 3.84 us
    psum x1 -> x0, waiting for transfers between devices: 110 us -> none  [per_device(): gsum = lax.psum(part_sum, 'wide')]
    all_to_all x0 -> x1, waiting for transfers between devices: none -> 8.96 us  [per_device(): lax.all_to_all(spread, 'wide', 0, 0)]
    all_to_all x0 -> x1, starting transfers between devices: none -> 8.19 us  [per_device(): lax.all_to_all(spread, 'wide', 0, 0)]
where the time goes in v1:
time: 35 us; the launch traced here: 34.6 us
  waiting for transfers between devices  8.96 us (26%)
  starting transfers between devices  8.19 us (23%)
  other arithmetic  5.27 us (15%)
  blocking collectives  4.05 us (12%)
  matrix products  3.84 us (11%)
  local copies, waits for them, and re-layouts  3.49 us (10%)
  between operations  0.79 us (2%)
    all_to_all x1, waiting for transfers between devices, per_device(): lax.all_to_all(spread, 'wide', 0, 0)  8.96 us
    all_to_all x1, starting transfers between devices, per_device(): lax.all_to_all(spread, 'wide', 0, 0)  8.19 us
    convert_element_type x1, local copies, waits for them, and re-layouts, per_device(): return (duals.astype(jnp.float32) - delta).astype(jnp.bfloat16)  2.63 us
    another operation x2, other arithmetic, per_device(): lax.linalg.triangular_solve(lower, forward - back, left_side=True, lower=...  2.55 us
    all_gather x1, blocking collectives, per_device(): cluster_vec = lax.all_gather(local, 'clus', axis=1, tiled=True)  2.1 us
    all_gather x1, blocking collectives, per_device(): beta = lax.all_gather(beta_part, 'clus', axis=1, tiled=True)  1.95 us
    dot_general x1, matrix products, per_device(): jnp.einsum('rsi,ski->rsk', duals, masked, preferred_element_type=jnp.floa...  1.86 us
    select_n x1, other arithmetic, per_device(): masked = jnp.where(active[:, None, :], kernel, jnp.zeros_like(kernel))  0.98 us
  transfers between devices with their start and end apart: 1, of which 1 were waited for; matrix products, arithmetic and copies ran while one was open for 0% of the time, Pallas kernels for 0%

profile of v1, /device:TPU:0, one launch (start us, length us, event | category | flops | bytes accessed | tf_op | source)
XLA Modules:
  0.0 34.6 jit_solution(7317522709146203964)
XLA Ops:
  0.0 0.0 copy-start
  0.7 0.7 %convert_bitcast_fusion = f32[24,1]{0,1:T(1,128)S(1)} fusion(s32[1,24]{1,0:T(1,128)} %param.12), kind=kLoop, calls=%fused_computation.28 | loop fusion | flops 24 | bytes 192 | tf_op jit(solution)/shard_map/convert_element_type | solution.py:24
  1.4 0.1 copy.30
  1.5 0.7 %fusion.18 = f32[1,24,24]{2,1,0:T(8,128)S(1)} fusion(f32[1,24,24]{2,1,0:T(8,128)} %param.11), kind=kLoop, calls=%fused_computation.25 | loop fusion | flops 1152 | bytes 4608 | tf_op jit(solution)/shard_map/triangular_solve | solution.py:39
  2.2 1.8 %custom-call.5 = f32[1,24,24]{1,2,0:T(8,128)S(1)} custom-call(f32[1,24,24]{2,1,0:T(8,128)S(1)} %fusion.18), custom_call_target="InvertDiagBlocksLowerTriangular" | custom-call | tf_op jit(solution)/shard_map/triangular_solve | solution.py:39
  4.0 0.8 %compare_and_fusion = pred[2,3840]{1,0:T(4,128)(4,1)S(1)} fusion(pred[2]{0:T(512)(128)(4,1)S(1)} %iota_compare_fusion.5, s32[2]{0:T(128)} %param.10), kind=kLoop, calls=%fused_computation.16 | loop fusion | flops 15360 | bytes 7690 | tf_op jit(solution)/shard_map/and | solution.py:13
  4.8 1.0 %broadcast_select_fusion = bf16[2,6,3840]{2,0,1:T(2,128)(2,1)S(1)} fusion(bf16[2,6,3840]{2,0,1:T(2,128)(2,1)} %param.8, pred[2,3840]{1,0:T(4,128)(4,1)S(1)} %compare_and_fusion), kind=kLoop, calls=%fused_computation.13 | loop fusion | flops 46080 | bytes 192000 | tf_op jit(solution)/shard_map/jit(_where)/select_n | solution.py:14
  5.8 0.0 copy-start.2
  5.8 1.9 %fusion.4 = f32[96,2,6]{0,2,1:T(8,128)S(1)} fusion(bf16[96,2,3840]{2,1,0:T(2,128)(2,1)} %param.7, bf16[2,6,3840]{2,0,1:T(2,128)(2,1)S(1)} %broadcast_select_fusion), kind=kOutput, calls=%fused_computation.6 | convolution fusion | flops 8847360 | bytes 1571328 | tf_op jit(solution)/shard_map/rsi,ski->rsk/dot_general | solution.py:15
  7.6 0.0 copy-start.1
  7.6 2.1 %all-gather = f32[2,12,96]{2,1,0:T(8,128)S(1)} all-gather(f32[1,12,96]{2,1,0:T(8,128)S(1)} %bitcast.36), channel_id=1, replica_groups=mesh['wide'=16,'clus'=2] {'clus'}, dimensions={0}, use_global_device_ids=true | all-gather | bytes 13824 | tf_op jit(solution)/shard_map/all_gather | solution.py:17
  9.7 0.2 fusion.16
  9.9 0.1 pad_maximum_fusion
  10.0 0.7 %broadcast_in_dim.14 = f32[16,24,97]{2,1,0:T(8,128)} broadcast(f32[24,97]{1,0:T(8,128)S(1)} %pad_maximum_fusion), dimensions={1,2} | broadcast | bytes 158304 | tf_op jit(solution)/shard_map/broadcast_in_dim | solution.py:25
  10.7 8.2 %all-to-all-start = ((f32[16,24,97]{2,1,0:T(8,128)}), f32[16,24,97]{2,1,0:T(8,128)S(1)}, u32[]{:S(2)}, u32[]{:S(2)}) async-start(f32[16,24,97]{2,1,0:T(8,128)} %broadcast_in_dim.14), calls=%async_computation | async-start | bytes 393216 | tf_op jit(solution)/shard_map/all_to_all | solution.py:26
  18.9 9.0 %all-to-all-done = f32[16,24,97]{2,1,0:T(8,128)S(1)} async-done(((f32[16,24,97]{2,1,0:T(8,128)}), f32[16,24,97]{2,1,0:T(8,128)S(1)}, u32[]{:S(2)}, u32[]{:S(2)}) %all-to-all-start) | async-done | bytes 149024 | tf_op jit(solution)/shard_map/all_to_all | solution.py:26
  27.9 0.2 fusion.9
  28.1 0.5 %fusion.7 = f32[96,384]{1,0:T(8,128)S(1)} fusion(s32[384]{0:T(512)S(1)} %fusion.9, f32[384,97]{1,0:T(8,128)S(1)} %bitcast.35), kind=kOutput, calls=%fused_computation.8 | convolution fusion | flops 170016768 | bytes 297984 | tf_op jit(solution)/shard_map/dot_general | solution.py:32
  28.6 0.0 copy-done
  28.6 0.4 %fusion.20 = f32[96,192]{0,1:T(8,128)S(1)} fusion(f32[96,384]{1,0:T(8,128)S(1)} %fusion.7, f32[384,192]{0,1:T(8,128)S(1)} %copy-done), kind=kOutput, calls=%fused_computation.30 | convolution fusion | flops 84934656 | bytes 516096 | tf_op jit(solution)/shard_map/dot_general | solution.py:33
  29.0 1.9 %all_gather.7 = f32[96,384]{0,1:T(8,128)S(1)} all-gather(f32[96,192]{0,1:T(8,128)S(1)} %fusion.20), channel_id=1, replica_groups=mesh['wide'=16,'clus'=2] {'clus'}, dimensions={1}, use_global_device_ids=true | all-gather | bytes 221184 | tf_op jit(solution)/shard_map/all_gather | solution.py:34
  31.0 0.0 copy-done.2
  31.0 0.2 convolution_subtract_fusion
  31.2 0.1 fusion.14
  31.4 0.0 copy-done.1
  31.4 0.6 %fusion.1 = bf16[96,2,3840]{2,0,1:T(8,128)(2,1)S(1)} fusion(bf16[96,2,6]{0,2,1:T(8,128)(2,1)S(1)} %convert_element_type.40, bf16[96,2,3840]{2,1,0:T(2,128)(2,1)S(1)} %copy-done.1, bf16[2,6,3840]{2,0,1:T(2,128)(2,1)S(1)} %broadcast_select_fusion), kind=kOutput, calls=%fused_computation.2 | convolution fusion | flops 11059200 | bytes 3043584 | tf_op jit(solution)/shard_map/rsk,ski->rsi/dot_general | solution.py:46
  32.0 2.6 %copy.33 = bf16[96,2,3840]{2,1,0:T(2,128)(2,1)} copy(bf16[96,2,3840]{2,0,1:T(8,128)(2,1)S(1)} %fusion.1) | data formatting | bytes 2949120 | tf_op jit(solution)/shard_map/convert_element_type | solution.py:47
  (5 shorter events, 0.1 us)
Async XLA Ops:
  0.0 28.6 %copy-start = (f32[384,192]{0,1:T(8,128)S(1)}, f32[384,192]{0,1:T(8,128)}, u32[]{:S(2)}) copy-start(f32[384,192]{0,1:T(8,128)} %param.13) | copy-start | bytes 884740
  5.8 25.2 %copy-start.2 = (s32[1,24]{1,0:T(1,128)S(1)}, s32[1,24]{1,0:T(1,128)}, u32[]{:S(2)}) copy-start(s32[1,24]{1,0:T(1,128)} %param.12) | copy-start | bytes 292
  7.6 23.8 %copy-start.1 = (bf16[96,2,3840]{2,1,0:T(2,128)(2,1)S(1)}, bf16[96,2,3840]{2,1,0:T(2,128)(2,1)}, u32[]{:S(2)}) copy-start(bf16[96,2,3840]{2,1,0:T(2,128)(2,1)} %param.7) | copy-start | bytes 4423684
  10.7 17.2 %all-to-all-start = ((f32[16,24,97]{2,1,0:T(8,128)}), f32[16,24,97]{2,1,0:T(8,128)S(1)}, u32[]{:S(2)}, u32[]{:S(2)}) async-start(f32[16,24,97]{2,1,0:T(8,128)} %broadcast_in_dim.14), calls=%async_computation | async-start | bytes 393216 | tf_op jit(solution)/shard_map/all_to_all | solution.py:26

commit v2 on v0

v2 whole, which is shorter than its diff:
```python
import functools

import jax
import jax.numpy as jnp
from jax import lax
from jax.experimental import pallas as pl
from jax.experimental.pallas import tpu as pltpu
from jax.sharding import PartitionSpec as P

F32 = jnp.float32
BF16 = jnp.bfloat16
LANES = 128
HI = lax.Precision.HIGHEST
NT = (((1,), (1,)), ((), ()))
NN = (((1,), (0,)), ((), ()))
VMEM = pl.BlockSpec(memory_space=pltpu.VMEM)
HBM = pl.BlockSpec(memory_space=pltpu.HBM)
FIRST_LIMIT = 60 * 2**20
LAST_LIMIT = 20 * 2**20


def iota(shape, dim):
    return lax.broadcasted_iota(jnp.int32, shape, dim)


def split(x, parts):
    out = []
    for n in range(parts):
        head = x.astype(BF16)
        out.append(head)
        if n + 1 < parts:
            x = x - head.astype(F32)
    return out


def dot(a, b, dims):
    return lax.dot_general(a, b, dims, preferred_element_type=F32)


def chunks_of(width):
    for count in (5, 3, 2):
        if width % (count * LANES) == 0:
            return count
    return 1


def rows_of_slots(sub, rhs, lanes):
    return (iota((rhs * sub, lanes), 0) // sub == iota((rhs * sub, lanes), 1)).astype(F32).astype(BF16)


def first_kernel(rhs, counts_ref, sizes_ref, kernel_ref, lower_ref, map_ref, duals_ref,
                 send_ref, masked_ref, inv_ref,
                 count_s, size_s, raw_ref, tri_ref, row_ref, x_ref, acc_ref, sol_ref, own_ref, sems, small_sems):
    modes, sub, width = kernel_ref.shape
    rows = modes * sub
    ck = lower_ref.shape[0]
    lanes = inv_ref.shape[1]
    count = chunks_of(width)
    step = width // count

    def copy(n):
        cols = pl.ds(n * step, step)
        return pltpu.make_async_copy(duals_ref.at[:, :, cols], x_ref.at[:, :, cols], sems.at[n])

    small = [
        pltpu.make_async_copy(src, dst, small_sems.at[n])
        for n, (src, dst) in enumerate(
            ((lower_ref, tri_ref), (map_ref, row_ref), (counts_ref, count_s), (sizes_ref, size_s), (kernel_ref, raw_ref))
        )
    ]
    for one in small:
        one.start()
    for n in range(count):
        copy(n).start()

    place = lax.axis_index("clus").astype(jnp.int32)
    small[0].wait()
    small[1].wait()
    upper = tri_ref[...].T
    sol = (iota((ck, lanes), 1) == rhs + iota((ck, lanes), 0)).astype(F32)
    row_id = iota((ck, 1), 0)
    for i in range(ck - 1, -1, -1):
        column = upper[:, i : i + 1]
        row = sol[i : i + 1, :] / upper[i : i + 1, i : i + 1]
        sol = jnp.where(row_id == i, row, sol - jnp.where(row_id < i, column, 0.0) * row)
    for c in range(lanes // LANES):
        cols = slice(c * LANES, (c + 1) * LANES)
        sol_ref[c] = sol[:, cols]
        for s in range(sub):
            own_ref[c, pl.ds(s, modes, stride=sub), :] = sol_ref[c, pl.ds(place * rows + s * modes, modes), :]
        inv_ref[:, cols] = own_ref[c]
    wanted = iota((rows, ck), 1) == place * rows + iota((rows, ck), 0)
    own_map = jnp.sum(jnp.where(wanted, row_ref[...].astype(F32), 0.0), axis=1, keepdims=True)

    for one in small[2:]:
        one.wait()
    slot = iota((rows, width), 0) % sub
    limit = jnp.zeros((rows, width), jnp.int32)
    for s in range(sub):
        size = jnp.where(s < count_s[0], size_s[s], 0)
        limit = jnp.where(slot == s, size, limit)
    values = raw_ref[...].reshape(rows, width).astype(F32)
    masked_ref[...] = jnp.where(iota((rows, width), 1) < limit, values, 0.0).astype(BF16)

    acc_ref[...] = jnp.zeros_like(acc_ref)
    for n in range(count):
        copy(n).wait()
        x = x_ref[:, :, n * step : (n + 1) * step].reshape(rhs * sub, step)
        acc_ref[...] += dot(masked_ref[:, n * step : (n + 1) * step], x, NT)
    same = iota((rows, rhs * sub), 0) % sub == iota((rows, rhs * sub), 1) % sub
    mixed = jnp.where(same, acc_ref[...], 0.0)
    pick = rows_of_slots(sub, rhs, lanes)
    local = sum(dot(part, pick, NN) for part in split(mixed, 3))
    block = local + inv_ref[...] + jnp.where(iota((rows, lanes), 1) == rhs + ck, own_map, 0.0)
    group = 2 if send_ref.shape[0] % (2 * rows) == 0 else 1
    block = jnp.concatenate([block] * group, axis=0)
    for d in range(send_ref.shape[0] // (rows * group)):
        send_ref[pl.ds(d * rows * group, rows * group), :] = block


def write_out(corr, masked_ref, x_ref, out_ref, o_ref, sems):
    rhs, sub, width = x_ref.shape
    rows = masked_ref.shape[0]
    count = chunks_of(width)
    step = width // count
    pick = rows_of_slots(sub, rhs, rhs)
    wide = dot(pick, corr, NT)
    same = iota((rhs * sub, rows), 0) % sub == iota((rhs * sub, rows), 1) % sub
    wide = jnp.where(same, wide, 0.0).astype(BF16)

    def copy(n):
        cols = pl.ds(n * step, step)
        return pltpu.make_async_copy(o_ref.at[:, :, cols], out_ref.at[:, :, cols], sems.at[n])

    for n in range(count):
        cols = slice(n * step, (n + 1) * step)
        x = x_ref[:, :, cols].reshape(rhs * sub, step).astype(F32)
        value = x - dot(wide, masked_ref[:, cols], NN)
        o_ref[:, :, cols] = value.astype(BF16).reshape(rhs, sub, step)
        copy(n).start()
    for n in range(count):
        copy(n).wait()


def last_kernel(rhs, ck, recv_ref, coarse_ref, own_ref, masked_ref, x_ref, out_ref, o_ref, block_ref, sems):
    total = recv_ref.shape[0]
    gk = coarse_ref.shape[1]
    target = recv_ref[:, rhs + ck : rhs + ck + 1].astype(jnp.int32)
    hot = (target == iota((total, gk), 1)).astype(F32).astype(BF16)
    taken = sum(dot(part, hot, NT) for part in split(coarse_ref[...], 3))
    block_ref[...] = jnp.zeros_like(block_ref)
    for w in range(total // ck):
        here = slice(w * ck, (w + 1) * ck)
        block_ref[here, here] = recv_ref[here, rhs : rhs + ck]
    left = own_ref[...] - taken
    left_hi, left_lo = split(left, 2)
    block_hi, block_lo = split(block_ref[...], 2)
    weight = dot(left_hi, block_hi, NT) + dot(left_lo, block_hi, NT) + dot(left_hi, block_lo, NT)
    weight_hi, weight_lo = split(weight, 2)
    local_hi, local_lo = split(recv_ref[:, :rhs], 2)
    corr = dot(weight_hi, local_hi, NN) + dot(weight_lo, local_hi, NN) + dot(weight_hi, local_lo, NN)
    write_out(corr.astype(BF16), masked_ref, x_ref, out_ref, o_ref, sems)


def last_kernel_plain(corr_ref, masked_ref, x_ref, out_ref, o_ref, sems):
    write_out(corr_ref[...].astype(BF16), masked_ref, x_ref, out_ref, o_ref, sems)


def per_device(duals, kernel, sub_counts, dual_sizes, cluster_factor, coarse_map, coarse_inverse):
    rhs, sub, width = duals.shape
    modes = kernel.shape[1]
    rows = sub * modes
    clusters = lax.axis_size("wide")
    members = lax.axis_size("clus")
    devices = clusters * members
    total = devices * rows
    ck = cluster_factor.shape[1]
    gk, own_cols = coarse_inverse.shape
    lanes = -(-(rhs + ck + 1) // LANES) * LANES
    count = chunks_of(width)
    place = lax.axis_index("clus").astype(jnp.int32)
    params = pltpu.CompilerParams(vmem_limit_bytes=LAST_LIMIT)

    send, masked, inv = pl.pallas_call(
        functools.partial(first_kernel, rhs),
        out_shape=(
            jax.ShapeDtypeStruct((total, lanes), F32),
            jax.ShapeDtypeStruct((rows, width), BF16),
            jax.ShapeDtypeStruct((rows, lanes), F32),
        ),
        in_specs=[HBM] * 6,
        out_specs=(VMEM, VMEM, VMEM),
        scratch_shapes=[
            pltpu.SMEM((1,), jnp.int32),
            pltpu.SMEM((sub,), jnp.int32),
            pltpu.VMEM((modes, sub, width), BF16),
            pltpu.VMEM((ck, ck), F32),
            pltpu.VMEM((1, ck), jnp.int32),
            pltpu.VMEM((rhs, sub, width), BF16),
            pltpu.VMEM((rows, rhs * sub), F32),
            pltpu.VMEM((lanes // LANES, ck, LANES), F32),
            pltpu.VMEM((lanes // LANES, rows, LANES), F32),
            pltpu.SemaphoreType.DMA((count,)),
            pltpu.SemaphoreType.DMA((5,)),
        ],
        compiler_params=pltpu.CompilerParams(vmem_limit_bytes=FIRST_LIMIT),
    )(sub_counts, dual_sizes, kernel.transpose(1, 0, 2), cluster_factor[0], coarse_map, duals)

    spread = send.reshape(devices, rows, lanes // LANES, LANES)
    recv = lax.all_to_all(spread, ("wide", "clus"), 0, 0)

    inv, rows_map, coarse_t, _ = lax.optimization_barrier((inv, coarse_map[0], coarse_inverse.T, send))
    hot = (rows_map[:, None] == place * own_cols + iota((ck, own_cols), 1)).astype(F32)
    part = jnp.dot(hot, coarse_t, precision=HI)
    picked = part
    for shift in range(1, members):
        picked = picked + lax.ppermute(part, "clus", [(i, (i + shift) % members) for i in range(members)])
    own_inv = inv[:, rhs : rhs + ck]
    coarse = jnp.dot(own_inv, picked, precision=HI)

    scratch = pltpu.VMEM((rhs, sub, width), BF16)
    sems = pltpu.SemaphoreType.DMA((count,))
    out_shape = jax.ShapeDtypeStruct(duals.shape, BF16)
    if total * max(total, gk) <= 2**20:
        cluster = iota((1, clusters, 1), 1) == lax.axis_index("wide")
        own = jnp.where(cluster, own_inv[:, None, :], 0.0).reshape(rows, total)
        return pl.pallas_call(
            functools.partial(last_kernel, rhs, ck),
            out_shape=out_shape,
            in_specs=[VMEM] * 5,
            out_specs=HBM,
            scratch_shapes=[scratch, pltpu.VMEM((total, total), F32), sems],
            compiler_params=params,
        )(recv.reshape(total, lanes), coarse, own, masked, duals)

    blocks = recv.reshape(clusters, ck, lanes)
    forward = jnp.einsum("wma,wmr->war", blocks[:, :, rhs : rhs + ck], blocks[:, :, :rhs], precision=HI)
    target = blocks[:, :, rhs + ck].astype(jnp.int32).reshape(total)
    all_hot = (target[:, None] == iota((total, gk), 1)).astype(F32)
    gsum = lax.dot_general(all_hot, forward.reshape(total, rhs), (((0,), (0,)), ((), ())), precision=HI)
    mine = lax.dynamic_index_in_dim(forward, lax.axis_index("wide"), 0, keepdims=False)
    corr = jnp.dot(own_inv, mine, precision=HI) - jnp.dot(coarse, gsum, precision=HI)
    return pl.pallas_call(
        last_kernel_plain,
        out_shape=out_shape,
        in_specs=[VMEM] * 3,
        out_specs=HBM,
        scratch_shapes=[scratch, sems],
        compiler_params=params,
    )(corr, masked, duals)


def solution(mesh):
    in_specs = (
        P(None, ("wide", "clus"), None),
        P(("wide", "clus"), None, None),
        P(("wide", "clus")),
        P(("wide", "clus")),
        P("wide", None, None),
        P("wide", None),
        P(None, "clus"),
    )
    out_specs = P(None, ("wide", "clus"), None)
    return jax.shard_map(
        per_device, mesh=mesh, in_specs=in_specs, out_specs=out_specs, check_vma=False
    )
```

time: 140 us -> 25.3 us (0.18)
  waiting for transfers between devices: 110 us -> 6.34 us
  between operations: 14.2 us -> 0.86 us
  starting transfers between devices: 0.01 us -> 7.64 us
  Pallas kernels: 0 us -> 6.88 us
  other arithmetic: 4.31 us -> 0.02 us
  matrix products: 5.34 us -> 1.16 us
  blocking collectives: 3.92 us -> 0 us
    psum x1 -> x0, waiting for transfers between devices: 110 us -> none  [per_device(): gsum = lax.psum(part_sum, 'wide')]
    all_to_all x0 -> x1, starting transfers between devices: none -> 7.33 us  [per_device(): recv = lax.all_to_all(spread, ('wide', 'clus'), 0, 0)]
    pallas_call x0 -> x2, Pallas kernels: none -> 6.88 us  [the longest x1 3.65 us: per_device(): pl.pallas_call(functools.partial(first_kernel, rhs), out_shape=(jax.Shape...]
    all_to_all x0 -> x1, waiting for transfers between devices: none -> 6.34 us  [per_device(): recv = lax.all_to_all(spread, ('wide', 'clus'), 0, 0)]
    all_gather x2 -> x0, blocking collectives: 3.92 us -> none  [the longest x1 1.97 us: per_device(): cluster_vec = lax.all_gather(local, 'clus', axis=1, tiled=True)]
    dot_general x5 -> x2, matrix products: 5.01 us -> 1.16 us  [the longest x1 0.92 us: per_device(): coarse = jnp.dot(own_inv, picked, precision=HI)]
    convert_element_type x3 -> x0, local copies, waits for them, and re-layouts: 2.67 us -> none  [the longest x1 2.63 us: per_device(): return (duals.astype(jnp.float32) - delta).astype(jnp.bfloat16)]
    another operation x2 -> x0, other arithmetic: 2.55 us -> none  [per_device(): lax.linalg.triangular_solve(lower, (forward - back).T, left_side=True, lo...]
  transfers between devices with their start and end apart: 1 -> 2, of which waited for: 1 -> 1; matrix products, arithmetic and copies ran while one was open for 0% -> 9% of each run, Pallas kernels for 0% -> 0%
where the time goes in v2:
time: 25.3 us; the launch traced here: 24.9 us
  starting transfers between devices  7.64 us (30%)
  Pallas kernels  6.88 us (27%)
  waiting for transfers between devices  6.34 us (25%)
  local copies, waits for them, and re-layouts  1.97 us (8%)
  matrix products  1.16 us (5%)
  between operations  0.86 us (3%)
    all_to_all x1, starting transfers between devices, per_device(): recv = lax.all_to_all(spread, ('wide', 'clus'), 0, 0)  7.33 us
    all_to_all x1, waiting for transfers between devices, per_device(): recv = lax.all_to_all(spread, ('wide', 'clus'), 0, 0)  6.34 us
    pallas_call x1, Pallas kernels, per_device(): pl.pallas_call(functools.partial(first_kernel, rhs), out_shape=(jax.Shape...  3.65 us
    pallas_call x1, Pallas kernels, per_device(): pl.pallas_call(functools.partial(last_kernel, rhs, ck), out_shape=out_sha...  3.23 us
    dot_general x1, matrix products, per_device(): coarse = jnp.dot(own_inv, picked, precision=HI)  0.92 us
    unnamed x8, local copies, waits for them, and re-layouts  0.91 us
    slice x1, local copies, waits for them, and re-layouts, per_device(): own_inv = inv[:, rhs:rhs + ck]  0.77 us
  transfers between devices with their start and end apart: 2, of which 1 were waited for; matrix products, arithmetic and copies ran while one was open for 9% of the time, Pallas kernels for 0%

profile of v2, /device:TPU:0, one launch (start us, length us, event | category | flops | bytes accessed | tf_op | source)
XLA Modules:
  0.0 24.9 jit_solution(7913990632458347956)
XLA Ops:
  0.0 0.0 copy-start
  0.0 0.0 copy-start.3
  0.0 0.0 copy-start.1
  0.8 3.6 %shard_map.73 = (f32[384,128]{1,0:T(8,128)}, bf16[12,3840]{1,0:T(8,128)(2,1)}, f32[12,128]{1,0:T(8,128)}) custom-call(s32[1]{0:T(128)S(6)} %copy.9.counts_ref, s32[2]{0:T(128)} %sizes_ref.1, bf16[6,2,3840]{2,1,0:T(2,128)(2,1)} %bitcast.10, f32[24,24]{1,0:T(8,128)} %bitcast.11, s32[1,24]{1,0:T(1,128)} %map_ref.1, bf16[96,2,3840]{2,1,0:T(2,128)(2,1)} %x_ref.1), custom_call_target="tpu_custom_call" | custom-call | tf_op jit(solution)/shard_map/pallas_call | solution.py:184
  4.4 7.3 %all-to-all-start = ((f32[32,12,1,128]{3,2,1,0:T(1,128)}), f32[32,12,1,128]{3,2,1,0:T(1,128)S(1)}, u32[]{:S(2)}, u32[]{:S(2)}) async-start(f32[32,12,1,128]{3,2,1,0:T(1,128)} %bitcast.9), calls=%async_computation | async-start | bytes 393216 | tf_op jit(solution)/shard_map/all_to_all | solution.py:210
  11.8 0.0 copy-done
  11.8 0.0 copy-done.3
  11.8 0.2 fusion.2
  12.1 0.3 %collective-permute-start = (f32[24,384]{1,0:T(8,128)S(1)}, f32[24,384]{1,0:T(8,128)S(1)}, u32[]{:S(2)}, u32[]{:S(2)}) collective-permute-start(f32[24,384]{1,0:T(8,128)S(1)} %fusion.2), channel_id=1, source_target_pairs={{0,1},{1,0},{2,3},{3,2},{4,5},{5,4},{6,7},{7,6},{8,9},{9,8},{10,11... | collective-permute-start | bytes 110600 | tf_op jit(solution)/shard_map/ppermute | solution.py:217
  12.4 0.1 broadcast_in_dim.28
  12.4 0.1 broadcast_in_dim.29
  12.5 0.8 %slice.3 = f32[12,24]{1,0:T(8,128)S(1)} slice(f32[12,128]{1,0:T(8,128)} %get-tuple-element.13), slice={[0:12], [96:120]} | slice | bytes 2304 | tf_op jit(solution)/shard_map/slice | solution.py:218
  13.3 0.1 broadcast_in_dim.32
  13.5 0.0 collective-permute-done
  13.5 0.9 %fusion.coarse_ref = f32[12,384]{1,0:T(8,128)S(1)} fusion(f32[24,384]{1,0:T(8,128)S(1)} %fusion.2, f32[24,384]{1,0:T(8,128)S(1)} %collective-permute-done, f32[12,128]{1,0:T(8,128)} %get-tuple-element.13), kind=kOutput, calls=%fused_computation | convolution fusion | flops 1336320 | bytes 98304 | tf_op jit(solution)/shard_map/dot_general | solution.py:219
  14.4 6.3 %all-to-all-done = f32[32,12,1,128]{3,2,1,0:T(1,128)S(1)} async-done(((f32[32,12,1,128]{3,2,1,0:T(1,128)}), f32[32,12,1,128]{3,2,1,0:T(1,128)S(1)}, u32[]{:S(2)}, u32[]{:S(2)}) %all-to-all-start) | async-done | bytes 196640 | tf_op jit(solution)/shard_map/all_to_all | solution.py:210
  20.7 0.0 copy-done.1
  20.7 0.0 copy-start.2
  20.7 0.9 %copy-done.2 = bf16[12,3840]{1,0:T(8,128)(2,1)S(1)} copy-done((bf16[12,3840]{1,0:T(8,128)(2,1)S(1)}, bf16[12,3840]{1,0:T(8,128)(2,1)}, u32[]{:S(2)}) %copy-start.2) | copy-done | bytes 92184
  21.6 3.2 %shard_map.74 = bf16[96,2,3840]{2,1,0:T(2,128)(2,1)} custom-call(f32[384,128]{1,0:T(8,128)S(1)} %bitcast.8, f32[12,384]{1,0:T(8,128)S(1)} %fusion.coarse_ref, f32[12,384]{1,0:T(8,128)S(1)} %broadcast_select_fusion.own_ref, bf16[12,3840]{1,0:T(8,128)(2,1)S(1)} %copy-done.2, bf16[96,2,3840]{2,1,0:T(2,128)(2,1)S(1)} %copy-done.1), custom_call_target="tpu_custom_call" | custom-call | tf_op jit(solution)/shard_map/pallas_call | solution.py:227
  (4 shorter events, 0.0 us)
Async XLA Ops:
  0.0 11.8 %copy-start = (f32[384,192]{0,1:T(8,128)S(1)}, f32[384,192]{0,1:T(8,128)}, u32[]{:S(2)}) copy-start(f32[384,192]{0,1:T(8,128)} %param.13) | copy-start | bytes 884740
  0.0 11.8 %copy-start.3 = (s32[1,24]{1,0:T(1,128)S(1)}, s32[1,24]{1,0:T(1,128)}, u32[]{:S(2)}) copy-start(s32[1,24]{1,0:T(1,128)} %map_ref.1) | copy-start | bytes 292
  0.0 20.7 %copy-start.1 = (bf16[96,2,3840]{2,1,0:T(2,128)(2,1)S(1)}, bf16[96,2,3840]{2,1,0:T(2,128)(2,1)}, u32[]{:S(2)}) copy-start(bf16[96,2,3840]{2,1,0:T(2,128)(2,1)} %x_ref.1) | copy-start | bytes 4423684
  4.4 16.3 %all-to-all-start = ((f32[32,12,1,128]{3,2,1,0:T(1,128)}), f32[32,12,1,128]{3,2,1,0:T(1,128)S(1)}, u32[]{:S(2)}, u32[]{:S(2)}) async-start(f32[32,12,1,128]{3,2,1,0:T(1,128)} %bitcast.9), calls=%async_computation | async-start | bytes 393216 | tf_op jit(solution)/shard_map/all_to_all | solution.py:210
  12.1 1.4 %collective-permute-start = (f32[24,384]{1,0:T(8,128)S(1)}, f32[24,384]{1,0:T(8,128)S(1)}, u32[]{:S(2)}, u32[]{:S(2)}) collective-permute-start(f32[24,384]{1,0:T(8,128)S(1)} %fusion.2), channel_id=1, source_target_pairs={{0,1},{1,0},{2,3},{3,2},{4,5},{5,4},{6,7},{7,6},{8,9},{9,8},{10,11... | collective-permute-start | bytes 110600 | tf_op jit(solution)/shard_map/ppermute | solution.py:217
  20.7 0.9 %copy-start.2 = (bf16[12,3840]{1,0:T(8,128)(2,1)S(1)}, bf16[12,3840]{1,0:T(8,128)(2,1)}, u32[]{:S(2)}) copy-start(bf16[12,3840]{1,0:T(8,128)(2,1)} %get-tuple-element.16.masked_ref) | copy-start | bytes 276484

commit v3 on v2

v3 whole, which is shorter than its diff:
```python
import functools

import jax
import jax.numpy as jnp
from jax import lax
from jax.experimental import pallas as pl
from jax.experimental.pallas import tpu as pltpu
from jax.sharding import PartitionSpec as P

F32 = jnp.float32
BF16 = jnp.bfloat16
LANES = 128
HI = lax.Precision.HIGHEST
NT = (((1,), (1,)), ((), ()))
NN = (((1,), (0,)), ((), ()))
VMEM = pl.BlockSpec(memory_space=pltpu.VMEM)
HBM = pl.BlockSpec(memory_space=pltpu.HBM)
FIRST_LIMIT = 60 * 2**20
LAST_LIMIT = 20 * 2**20


def iota(shape, dim):
    return lax.broadcasted_iota(jnp.int32, shape, dim)


def stay(x):
    return pltpu.with_memory_space_constraint(x, pltpu.HBM)


def up(value, step):
    return -(-value // step) * step


def split(x, parts):
    out = []
    for n in range(parts):
        head = x.astype(BF16)
        out.append(head)
        if n + 1 < parts:
            x = x - head.astype(F32)
    return out


def dot(a, b, dims):
    return lax.dot_general(a, b, dims, preferred_element_type=F32)


def dot_parts(a, b, dims):
    a_hi, a_lo = split(a, 2)
    b_hi, b_lo = split(b, 2)
    rows = a.shape[0]
    both = dot(jnp.concatenate([a_hi, a_lo], axis=0), b_hi, dims)
    return both[:rows] + both[rows:] + dot(a_hi, b_lo, dims)


def dot_exact(a, hot, dims):
    rows = a.shape[0]
    parts = dot(jnp.concatenate(split(a, 3), axis=0), hot, dims)
    return parts[:rows] + parts[rows : 2 * rows] + parts[2 * rows :]


def chunks_of(width):
    for count in (5, 3, 2):
        if width % (count * LANES) == 0:
            return count
    return 1


def rows_of_slots(sub, rhs, lanes):
    return (iota((rhs * sub, lanes), 0) // sub == iota((rhs * sub, lanes), 1)).astype(F32).astype(BF16)


def slab_copies(whole_ref, slabs_ref, sems, back=False):
    count, rows, step = slabs_ref.shape
    flat = whole_ref.reshape(rows, count * step)

    def copy(n):
        part = flat.at[:, pl.ds(n * step, step)]
        ends = (slabs_ref.at[n], part) if back else (part, slabs_ref.at[n])
        return pltpu.make_async_copy(*ends, sems.at[n])

    return copy


def mask_kernel(raw_ref, count_s, size_s, sub):
    rows, width = raw_ref.shape
    slot = iota((rows, width), 0) % sub
    limit = jnp.zeros((rows, width), jnp.int32)
    for s in range(sub):
        size = jnp.where(s < count_s[0, 0], size_s[s], 0)
        limit = jnp.where(slot == s, size, limit)
    return jnp.where(iota((rows, width), 1) < limit, raw_ref[...].astype(F32), 0.0).astype(BF16)


def first_kernel(rhs, counts_ref, sizes_ref, kernel_ref, lower_ref, map_ref, duals_ref,
                 send_ref, inv_ref,
                 count_s, size_s, raw_ref, tri_ref, row_ref, x_ref, acc_ref, mix_ref, block_ref, sol_ref, sems, small_sems):
    modes, sub, width = kernel_ref.shape
    rows = modes * sub
    ck = lower_ref.shape[0]
    lanes = inv_ref.shape[1]
    count, _, step = x_ref.shape
    copy = slab_copies(duals_ref, x_ref, sems)
    small = [
        pltpu.make_async_copy(src, dst, small_sems.at[n])
        for n, (src, dst) in enumerate(
            (
                (lower_ref, tri_ref),
                (map_ref, row_ref),
                (counts_ref, count_s),
                (sizes_ref, size_s),
                (kernel_ref.reshape(rows, width), raw_ref),
            )
        )
    ]
    for one in small:
        one.start()
    for n in range(count):
        copy(n).start()

    place = lax.axis_index("clus").astype(jnp.int32)
    small[0].wait()
    small[1].wait()
    lower = tri_ref[...]
    eye = iota((ck, ck), 0) == iota((ck, ck), 1)
    scale = 1.0 / jnp.sum(jnp.where(eye, lower, 0.0), axis=1, keepdims=True)
    below = jnp.where(iota((ck, ck), 0) > iota((ck, ck), 1), lower * scale, 0.0)
    sol = jnp.where(iota((ck, lanes), 1) == rhs + iota((ck, lanes), 0), scale, 0.0)
    for i in range(ck - 1):
        sol = sol - below[:, i : i + 1] * sol[i : i + 1, :]
    inv_ref[...] = sol
    wanted = iota((rows, ck), 1) == place * rows + iota((rows, ck), 0)
    own_map = jnp.sum(jnp.where(wanted, row_ref[...].astype(F32), 0.0), axis=1, keepdims=True)
    for c in range(lanes // LANES):
        cols = slice(c * LANES, (c + 1) * LANES)
        sol_ref[c] = sol[:, cols]
        block_ref[:, cols] = sol_ref[c, pl.ds(place * rows, rows), :]
    block_ref[...] += jnp.where(iota((rows, lanes), 1) == rhs + ck, own_map, 0.0)

    for one in small[2:]:
        one.wait()
    masked = mask_kernel(raw_ref, count_s, size_s, sub)
    acc_ref[...] = jnp.zeros_like(acc_ref)
    total = jnp.zeros((rows, rhs * sub), F32)
    for n in range(count):
        copy(n).wait()
        total = total + dot(masked[:, n * step : (n + 1) * step], x_ref[n], NT)
    same = iota((rows, rhs * sub), 0) % sub == iota((rows, rhs * sub), 1) % sub
    acc_ref[:rows, :] = jnp.where(same, total, 0.0)
    mixed = dot_exact(acc_ref[...], rows_of_slots(sub, rhs, lanes), NN)
    for c in range(lanes // LANES):
        cols = slice(c * LANES, (c + 1) * LANES)
        mix_ref[c] = mixed[:, cols]
        for s in range(sub):
            here = slice(s * modes, (s + 1) * modes)
            block_ref[here, cols] += mix_ref[c, pl.ds(s, modes, stride=sub), :]
    group = 2 if send_ref.shape[0] % (2 * rows) == 0 else 1
    block = jnp.concatenate([block_ref[...]] * group, axis=0)
    for d in range(send_ref.shape[0] // (rows * group)):
        send_ref[pl.ds(d * rows * group, rows * group), :] = block


def middle_kernel(rhs, modes, inv_ref, picked_ref, coarse_ref, turned_ref, turn_ref):
    ck = picked_ref.shape[0]
    members = lax.axis_size("clus")
    rows = ck // members
    sub = rows // modes
    place = lax.axis_index("clus").astype(jnp.int32)
    turn_ref[...] = inv_ref[:, rhs : rhs + ck].T
    turned_ref[...] = jnp.zeros_like(turned_ref)
    for s in range(sub):
        turned_ref[pl.ds(s, modes, stride=sub), :] = turn_ref[pl.ds(place * rows + s * modes, modes), :]
    coarse_ref[...] = lax.dot_general(turned_ref[...], picked_ref[...], NN, precision=HI, preferred_element_type=F32)


def write_out(corr_of, counts_ref, sizes_ref, kernel_ref, duals_ref, out_ref,
              count_s, size_s, raw_ref, x_ref, o_ref, in_sems, out_sems, small_sems):
    modes, sub, width = kernel_ref.shape
    rows = modes * sub
    count, flat, step = x_ref.shape
    rhs = flat // sub
    in_copy = slab_copies(duals_ref, x_ref, in_sems)
    out_copy = slab_copies(out_ref, o_ref, out_sems, back=True)
    small = [
        pltpu.make_async_copy(src, dst, small_sems.at[n])
        for n, (src, dst) in enumerate(
            ((counts_ref, count_s), (sizes_ref, size_s), (kernel_ref.reshape(rows, width), raw_ref))
        )
    ]
    for one in small:
        one.start()
    for n in range(count):
        in_copy(n).start()
    corr = corr_of().astype(BF16)
    for one in small:
        one.wait()
    masked = mask_kernel(raw_ref, count_s, size_s, sub)
    wide = dot(rows_of_slots(sub, rhs, rhs), corr, NT)
    same = iota(wide.shape, 0) % sub == iota(wide.shape, 1) % sub
    wide = jnp.where(same, wide, 0.0)[:, :rows].astype(BF16)
    for n in range(count):
        in_copy(n).wait()
        delta = dot(wide, masked[:, n * step : (n + 1) * step], NN)
        o_ref[n] = (x_ref[n].astype(F32) - delta).astype(BF16)
        out_copy(n).start()
    for n in range(count):
        out_copy(n).wait()


def last_kernel(rhs, recv_ref, coarse_ref, turned_ref, counts_ref, sizes_ref, kernel_ref, duals_ref, out_ref,
                block_ref, sum_ref, *rest):
    def corr_of():
        total = recv_ref.shape[0]
        gk = coarse_ref.shape[1]
        ck = turned_ref.shape[1]
        cluster = lax.axis_index("wide").astype(jnp.int32)
        block_ref[...] = jnp.zeros_like(block_ref)
        for w in range(total // ck):
            here = slice(w * ck, (w + 1) * ck)
            block_ref[here, here] = recv_ref[here, rhs : rhs + ck]
        forward = dot_parts(block_ref[...], recv_ref[:, :rhs], NN)
        target = recv_ref[:, rhs + ck : rhs + ck + 1].astype(jnp.int32)
        hot = (target == iota((total, gk), 1)).astype(F32).astype(BF16)
        taken = dot_exact(coarse_ref[...], hot, NT)
        sum_ref[...] = forward
        mine = sum_ref[pl.ds(pl.multiple_of(cluster * ck, ck), ck), :]
        return dot_parts(turned_ref[...], mine, NN) - dot_parts(taken, forward, NN)

    write_out(corr_of, counts_ref, sizes_ref, kernel_ref, duals_ref, out_ref, *rest)


def last_kernel_plain(corr_ref, counts_ref, sizes_ref, kernel_ref, duals_ref, out_ref, *rest):
    write_out(lambda: corr_ref[...], counts_ref, sizes_ref, kernel_ref, duals_ref, out_ref, *rest)


def per_device(duals, kernel, sub_counts, dual_sizes, cluster_factor, coarse_map, coarse_inverse):
    rhs, sub, width = duals.shape
    modes = kernel.shape[1]
    rows = sub * modes
    padded = up(rows, 16)
    clusters = lax.axis_size("wide")
    members = lax.axis_size("clus")
    devices = clusters * members
    total = devices * rows
    ck = cluster_factor.shape[1]
    gk, own_cols = coarse_inverse.shape
    lanes = up(rhs + ck + 1, LANES)
    count = chunks_of(width)
    step = width // count
    place = lax.axis_index("clus").astype(jnp.int32)
    counts = sub_counts.reshape(1, 1)
    sizes = stay(dual_sizes)
    modes_first = stay(kernel.transpose(1, 0, 2))
    vectors = stay(duals)
    slabs = (count, rhs * sub, step)

    send, inv = pl.pallas_call(
        functools.partial(first_kernel, rhs),
        out_shape=(jax.ShapeDtypeStruct((total, lanes), F32), jax.ShapeDtypeStruct((ck, lanes), F32)),
        in_specs=[HBM] * 6,
        out_specs=(VMEM, VMEM),
        scratch_shapes=[
            pltpu.SMEM((1, 1), jnp.int32),
            pltpu.SMEM((sub,), jnp.int32),
            pltpu.VMEM((rows, width), BF16),
            pltpu.VMEM((ck, ck), F32),
            pltpu.VMEM((1, ck), jnp.int32),
            pltpu.VMEM(slabs, BF16),
            pltpu.VMEM((padded, rhs * sub), F32),
            pltpu.VMEM((lanes // LANES, padded, LANES), F32),
            pltpu.VMEM((rows, lanes), F32),
            pltpu.VMEM((lanes // LANES, ck, LANES), F32),
            pltpu.SemaphoreType.DMA((count,)),
            pltpu.SemaphoreType.DMA((5,)),
        ],
        compiler_params=pltpu.CompilerParams(vmem_limit_bytes=FIRST_LIMIT),
    )(counts, sizes, modes_first, stay(cluster_factor[0]), stay(coarse_map), vectors)

    spread = send.reshape(devices, rows, lanes // LANES, LANES)
    recv = lax.all_to_all(spread, ("wide", "clus"), 0, 0)

    inv, rows_map, coarse_t, _ = lax.optimization_barrier((inv, coarse_map[0], coarse_inverse.T, send))
    hot = (rows_map[:, None] == place * own_cols + iota((ck, own_cols), 1)).astype(F32)
    part = jnp.dot(hot, coarse_t, precision=HI)
    picked = part
    for shift in range(1, members):
        picked = picked + lax.ppermute(part, "clus", [(i, (i + shift) % members) for i in range(members)])
    params = pltpu.CompilerParams(vmem_limit_bytes=LAST_LIMIT)
    coarse, turned = pl.pallas_call(
        functools.partial(middle_kernel, rhs, modes),
        out_shape=(jax.ShapeDtypeStruct((padded, gk), F32), jax.ShapeDtypeStruct((padded, ck), F32)),
        in_specs=[VMEM, VMEM],
        out_specs=(VMEM, VMEM),
        scratch_shapes=[pltpu.VMEM((ck, ck), F32)],
        compiler_params=params,
    )(inv, picked)

    out_shape = jax.ShapeDtypeStruct(duals.shape, BF16)
    scratch = [
        pltpu.SMEM((1, 1), jnp.int32),
        pltpu.SMEM((sub,), jnp.int32),
        pltpu.VMEM((rows, width), BF16),
        pltpu.VMEM(slabs, BF16),
        pltpu.VMEM(slabs, BF16),
        pltpu.SemaphoreType.DMA((count,)),
        pltpu.SemaphoreType.DMA((count,)),
        pltpu.SemaphoreType.DMA((3,)),
    ]
    if total * max(total, gk) <= 2**20:
        return pl.pallas_call(
            functools.partial(last_kernel, rhs),
            out_shape=out_shape,
            in_specs=[VMEM] * 3 + [HBM] * 4,
            out_specs=HBM,
            scratch_shapes=[pltpu.VMEM((total, total), F32), pltpu.VMEM((total, rhs), F32), *scratch],
            compiler_params=params,
        )(recv.reshape(total, lanes), coarse, turned, counts, sizes, modes_first, vectors)

    blocks = recv.reshape(clusters, ck, lanes)
    forward = jnp.einsum("wam,wmr->war", blocks[:, :, rhs : rhs + ck], blocks[:, :, :rhs], precision=HI)
    target = blocks[:, :, rhs + ck].astype(jnp.int32).reshape(total)
    all_hot = (target[:, None] == iota((total, gk), 1)).astype(F32)
    gsum = lax.dot_general(all_hot, forward.reshape(total, rhs), (((0,), (0,)), ((), ())), precision=HI)
    mine = lax.dynamic_index_in_dim(forward, lax.axis_index("wide"), 0, keepdims=False)
    corr = jnp.dot(turned, mine, precision=HI) - jnp.dot(coarse, gsum, precision=HI)
    return pl.pallas_call(
        last_kernel_plain,
        out_shape=out_shape,
        in_specs=[VMEM] + [HBM] * 4,
        out_specs=HBM,
        scratch_shapes=scratch,
        compiler_params=params,
    )(corr, counts, sizes, modes_first, vectors)


def solution(mesh):
    in_specs = (
        P(None, ("wide", "clus"), None),
        P(("wide", "clus"), None, None),
        P(("wide", "clus")),
        P(("wide", "clus")),
        P("wide", None, None),
        P("wide", None),
        P(None, "clus"),
    )
    out_specs = P(None, ("wide", "clus"), None)
    return jax.shard_map(
        per_device, mesh=mesh, in_specs=in_specs, out_specs=out_specs, check_vma=False
    )
```

time: 25.3 us -> 23.5 us (0.929)
  local copies, waits for them, and re-layouts: 1.97 us -> 0.71 us
  waiting for transfers between devices: 6.34 us -> 7.38 us
  matrix products: 1.16 us -> 0.23 us
  Pallas kernels: 6.88 us -> 6.32 us
    ppermute x1, waiting for transfers between devices: 0.01 us -> 0.96 us  [per_device(): lax.ppermute(part, 'clus', [(i, (i + shift) % members) for i in range(mem...]
    dot_general x1 -> x0, matrix products: 0.92 us -> none  [per_device(): coarse = jnp.dot(own_inv, picked, precision=HI)]
    slice x1 -> x0, local copies, waits for them, and re-layouts: 0.77 us -> none  [per_device(): own_inv = inv[:, rhs:rhs + ck]]
    pallas_call x1, Pallas kernels: 3.65 us -> 3.02 us  [per_device(): pl.pallas_call(functools.partial(first_kernel, rhs), out_shape=(jax.Shape...]
    broadcast_in_dim x4 -> x0, local copies, waits for them, and re-layouts: 0.29 us -> none  [per_device(): own = jnp.where(cluster, own_inv[:, None, :], 0.0).reshape(rows, total)]
    unnamed x8 -> x6, local copies, waits for them, and re-layouts: 0.91 us -> 0.71 us
    pallas_call x1 -> x2, Pallas kernels: 3.23 us -> 3.31 us  [the longest x1 3.04 us: per_device(): pl.pallas_call(functools.partial(last_kernel, rhs), out_shape=out_shape,...]
  transfers between devices with their start and end apart: 2 -> 2, of which waited for: 1 -> 2; matrix products, arithmetic and copies ran while one was open for 9% -> 1% of each run, Pallas kernels for 0% -> 1%
where the time goes in v3:
time: 23.5 us; the launch traced here: 23.1 us
  starting transfers between devices  7.64 us (33%)
  waiting for transfers between devices  7.38 us (31%)
  Pallas kernels  6.32 us (27%)
  between operations  0.75 us (3%)
  local copies, waits for them, and re-layouts  0.71 us (3%)
    all_to_all x1, starting transfers between devices, per_device(): recv = lax.all_to_all(spread, ('wide', 'clus'), 0, 0)  7.33 us
    all_to_all x1, waiting for transfers between devices, per_device(): recv = lax.all_to_all(spread, ('wide', 'clus'), 0, 0)  6.42 us
    pallas_call x1, Pallas kernels, per_device(): pl.pallas_call(functools.partial(last_kernel, rhs), out_shape=out_shape,...  3.04 us
    pallas_call x1, Pallas kernels, per_device(): pl.pallas_call(functools.partial(first_kernel, rhs), out_shape=(jax.Shape...  3.02 us
    ppermute x1, waiting for transfers between devices, per_device(): lax.ppermute(part, 'clus', [(i, (i + shift) % members) for i in range(mem...  0.96 us
    unnamed x6, local copies, waits for them, and re-layouts  0.71 us
  transfers between devices with their start and end apart: 2, of which 2 were waited for; matrix products, arithmetic and copies ran while one was open for 1% of the time, Pallas kernels for 1%

profile of v3, /device:TPU:0, one launch (start us, length us, event | category | flops | bytes accessed | tf_op | source)
XLA Modules:
  0.0 23.1 jit_solution(231551990145380674)
XLA Ops:
  0.0 0.0 copy-start
  0.0 0.0 copy-start.2
  0.7 3.0 %shard_map.73 = (f32[384,128]{1,0:T(8,128)}, f32[24,128]{1,0:T(8,128)}) custom-call(s32[1,1]{1,0:T(1,128)} %bitcast.8.counts_ref, s32[2]{0:T(128)} %sizes_ref.3, bf16[6,2,3840]{2,1,0:T(2,128)(2,1)} %bitcast.12, f32[24,24]{1,0:T(8,128)} %bitcast.15, s32[1,24]{1,0:T(1,128)} %map_ref.1, bf16[96,2,3840]{2,1,0:T(2,128)(2,1)} %duals_ref.3), custom_call_target="tpu_custom_call" | custom-call | tf_op jit(solution)/shard_map/pallas_call | solution.py:257
  3.7 7.3 %all-to-all-start = ((f32[32,12,1,128]{3,2,1,0:T(1,128)}), f32[32,12,1,128]{3,2,1,0:T(1,128)S(1)}, u32[]{:S(2)}, u32[]{:S(2)}) async-start(f32[32,12,1,128]{3,2,1,0:T(1,128)} %bitcast.14), calls=%async_computation | async-start | bytes 393216 | tf_op jit(solution)/shard_map/all_to_all | solution.py:280
  11.1 0.0 copy-done
  11.1 0.0 copy-done.2
  11.1 0.2 %fusion = f32[24,384]{1,0:T(8,128)S(1)} fusion(f32[192,384]{1,0:T(8,128)S(1)} %bitcast.10, s32[192]{0:T(256)S(1)} %iota_add_fusion, s32[24]{0:T(128)S(1)} %bitcast.16), kind=kOutput, calls=%fused_computation | convolution fusion | flops 21238272 | bytes 332640 | tf_op jit(solution)/shard_map/dot_general | solution.py:284
  11.3 0.3 %collective-permute-start = (f32[24,384]{1,0:T(8,128)S(1)}, f32[24,384]{1,0:T(8,128)S(1)}, u32[]{:S(2)}, u32[]{:S(2)}) collective-permute-start(f32[24,384]{1,0:T(8,128)S(1)} %fusion), channel_id=1, source_target_pairs={{0,1},{1,0},{2,3},{3,2},{4,5},{5,4},{6,7},{7,6},{8,9},{9,8},{10,11... | collective-permute-start | bytes 110600 | tf_op jit(solution)/shard_map/ppermute | solution.py:287
  11.6 1.0 %collective-permute-done = f32[24,384]{1,0:T(8,128)S(1)} collective-permute-done((f32[24,384]{1,0:T(8,128)S(1)}, f32[24,384]{1,0:T(8,128)S(1)}, u32[]{:S(2)}, u32[]{:S(2)}) %collective-permute-start) | collective-permute-done | bytes 36896 | tf_op jit(solution)/shard_map/ppermute | solution.py:287
  12.6 0.0 copy-start.1
  12.6 0.7 %copy-done.1 = f32[24,128]{1,0:T(8,128)S(1)} copy-done((f32[24,128]{1,0:T(8,128)S(1)}, f32[24,128]{1,0:T(8,128)}, u32[]{:S(2)}) %copy-start.1) | copy-done | bytes 12312
  13.3 0.3 %shard_map.74 = (f32[16,384]{1,0:T(8,128)S(1)}, f32[16,24]{1,0:T(8,128)S(1)}) custom-call(f32[24,128]{1,0:T(8,128)S(1)} %copy-done.1, f32[24,384]{1,0:T(8,128)S(1)} %add.12.picked_ref), custom_call_target="tpu_custom_call" | custom-call | tf_op jit(solution)/shard_map/pallas_call | solution.py:289
  13.6 6.4 %all-to-all-done = f32[32,12,1,128]{3,2,1,0:T(1,128)S(1)} async-done(((f32[32,12,1,128]{3,2,1,0:T(1,128)}), f32[32,12,1,128]{3,2,1,0:T(1,128)S(1)}, u32[]{:S(2)}, u32[]{:S(2)}) %all-to-all-start) | async-done | bytes 196640 | tf_op jit(solution)/shard_map/all_to_all | solution.py:280
  20.0 3.0 %shard_map.75 = bf16[96,2,3840]{2,1,0:T(2,128)(2,1)} custom-call(f32[384,128]{1,0:T(8,128)S(1)} %bitcast.11, f32[16,384]{1,0:T(8,128)S(1)} %get-tuple-element.17.coarse_ref, f32[16,24]{1,0:T(8,128)S(1)} %get-tuple-element.18.turned_ref, s32[1,1]{1,0:T(1,128)} %bitcast.9.counts_ref, s32[2]{0:T(128)} %sizes_ref.3, bf16[6,2,3840]{2,1,0:T(2,128)(2,1)} %bitcast.13, ...), custom_call_target="tpu_custom_call" | custom-call | tf_op jit(solution)/shard_map/pallas_call | solution.py:310
  (2 shorter events, 0.0 us)
Async XLA Ops:
  0.0 11.1 %copy-start = (f32[384,192]{0,1:T(8,128)S(1)}, f32[384,192]{0,1:T(8,128)}, u32[]{:S(2)}) copy-start(f32[384,192]{0,1:T(8,128)} %param.13) | copy-start | bytes 884740
  0.0 11.1 %copy-start.2 = (s32[1,24]{1,0:T(1,128)S(1)}, s32[1,24]{1,0:T(1,128)}, u32[]{:S(2)}) copy-start(s32[1,24]{1,0:T(1,128)} %map_ref.1) | copy-start | bytes 292
  3.7 16.3 %all-to-all-start = ((f32[32,12,1,128]{3,2,1,0:T(1,128)}), f32[32,12,1,128]{3,2,1,0:T(1,128)S(1)}, u32[]{:S(2)}, u32[]{:S(2)}) async-start(f32[32,12,1,128]{3,2,1,0:T(1,128)} %bitcast.14), calls=%async_computation | async-start | bytes 393216 | tf_op jit(solution)/shard_map/all_to_all | solution.py:280
  11.3 1.3 %collective-permute-start = (f32[24,384]{1,0:T(8,128)S(1)}, f32[24,384]{1,0:T(8,128)S(1)}, u32[]{:S(2)}, u32[]{:S(2)}) collective-permute-start(f32[24,384]{1,0:T(8,128)S(1)} %fusion), channel_id=1, source_target_pairs={{0,1},{1,0},{2,3},{3,2},{4,5},{5,4},{6,7},{7,6},{8,9},{9,8},{10,11... | collective-permute-start | bytes 110600 | tf_op jit(solution)/shard_map/ppermute | solution.py:287
  12.6 0.7 %copy-start.1 = (f32[24,128]{1,0:T(8,128)S(1)}, f32[24,128]{1,0:T(8,128)}, u32[]{:S(2)}) copy-start(f32[24,128]{1,0:T(8,128)} %get-tuple-element.14.inv_ref) | copy-start | bytes 36868

commit v4 on v3

--- a/solution.py
+++ b/solution.py
@@ -160,27 +160,14 @@
         send_ref[pl.ds(d * rows * group, rows * group), :] = block
 
 
-def middle_kernel(rhs, modes, inv_ref, picked_ref, coarse_ref, turned_ref, turn_ref):
-    ck = picked_ref.shape[0]
-    members = lax.axis_size("clus")
-    rows = ck // members
-    sub = rows // modes
-    place = lax.axis_index("clus").astype(jnp.int32)
-    turn_ref[...] = inv_ref[:, rhs : rhs + ck].T
-    turned_ref[...] = jnp.zeros_like(turned_ref)
-    for s in range(sub):
-        turned_ref[pl.ds(s, modes, stride=sub), :] = turn_ref[pl.ds(place * rows + s * modes, modes), :]
-    coarse_ref[...] = lax.dot_general(turned_ref[...], picked_ref[...], NN, precision=HI, preferred_element_type=F32)
-
-
-def write_out(corr_of, counts_ref, sizes_ref, kernel_ref, duals_ref, out_ref,
-              count_s, size_s, raw_ref, x_ref, o_ref, in_sems, out_sems, small_sems):
+def middle_kernel(rhs, inv_ref, picked_ref, counts_ref, sizes_ref, kernel_ref, duals_ref,
+                  coarse_ref, turned_ref, masked_ref, x_ref,
+                  count_s, size_s, raw_ref, turn_ref, sems, small_sems):
     modes, sub, width = kernel_ref.shape
     rows = modes * sub
-    count, flat, step = x_ref.shape
-    rhs = flat // sub
-    in_copy = slab_copies(duals_ref, x_ref, in_sems)
-    out_copy = slab_copies(out_ref, o_ref, out_sems, back=True)
+    ck = picked_ref.shape[0]
+    count = x_ref.shape[0]
+    copy = slab_copies(duals_ref, x_ref, sems)
     small = [
         pltpu.make_async_copy(src, dst, small_sems.at[n])
         for n, (src, dst) in enumerate(
@@ -190,47 +177,57 @@
     for one in small:
         one.start()
     for n in range(count):
-        in_copy(n).start()
-    corr = corr_of().astype(BF16)
+        copy(n).start()
+    place = lax.axis_index("clus").astype(jnp.int32)
+    turn_ref[...] = inv_ref[:, rhs : rhs + ck].T
+    turned_ref[...] = jnp.zeros_like(turned_ref)
+    for s in range(sub):
+        turned_ref[pl.ds(s, modes, stride=sub), :] = turn_ref[pl.ds(place * rows + s * modes, modes), :]
+    coarse_ref[...] = lax.dot_general(turned_ref[...], picked_ref[...], NN, precision=HI, preferred_element_type=F32)
     for one in small:
         one.wait()
-    masked = mask_kernel(raw_ref, count_s, size_s, sub)
+    masked_ref[...] = mask_kernel(raw_ref, count_s, size_s, sub)
+    for n in range(count):
+        copy(n).wait()
+
+
+def write_out(corr, sub, masked_ref, x_ref, out_ref, o_ref, sems):
+    rows = masked_ref.shape[0]
+    count, flat, step = x_ref.shape
+    rhs = flat // sub
+    copy = slab_copies(out_ref, o_ref, sems, back=True)
     wide = dot(rows_of_slots(sub, rhs, rhs), corr, NT)
     same = iota(wide.shape, 0) % sub == iota(wide.shape, 1) % sub
     wide = jnp.where(same, wide, 0.0)[:, :rows].astype(BF16)
     for n in range(count):
-        in_copy(n).wait()
-        delta = dot(wide, masked[:, n * step : (n + 1) * step], NN)
+        delta = dot(wide, masked_ref[:, n * step : (n + 1) * step], NN)
         o_ref[n] = (x_ref[n].astype(F32) - delta).astype(BF16)
-        out_copy(n).start()
-    for n in range(count):
-        out_copy(n).wait()
-
-
-def last_kernel(rhs, recv_ref, coarse_ref, turned_ref, counts_ref, sizes_ref, kernel_ref, duals_ref, out_ref,
-                block_ref, sum_ref, *rest):
-    def corr_of():
-        total = recv_ref.shape[0]
-        gk = coarse_ref.shape[1]
-        ck = turned_ref.shape[1]
-        cluster = lax.axis_index("wide").astype(jnp.int32)
-        block_ref[...] = jnp.zeros_like(block_ref)
-        for w in range(total // ck):
-            here = slice(w * ck, (w + 1) * ck)
-            block_ref[here, here] = recv_ref[here, rhs : rhs + ck]
-        forward = dot_parts(block_ref[...], recv_ref[:, :rhs], NN)
-        target = recv_ref[:, rhs + ck : rhs + ck + 1].astype(jnp.int32)
-        hot = (target == iota((total, gk), 1)).astype(F32).astype(BF16)
-        taken = dot_exact(coarse_ref[...], hot, NT)
-        sum_ref[...] = forward
-        mine = sum_ref[pl.ds(pl.multiple_of(cluster * ck, ck), ck), :]
-        return dot_parts(turned_ref[...], mine, NN) - dot_parts(taken, forward, NN)
-
-    write_out(corr_of, counts_ref, sizes_ref, kernel_ref, duals_ref, out_ref, *rest)
-
-
-def last_kernel_plain(corr_ref, counts_ref, sizes_ref, kernel_ref, duals_ref, out_ref, *rest):
-    write_out(lambda: corr_ref[...], counts_ref, sizes_ref, kernel_ref, duals_ref, out_ref, *rest)
+        copy(n).start()
+    for n in range(count):
+        copy(n).wait()
+
+
+def last_kernel(rhs, sub, recv_ref, coarse_ref, turned_ref, masked_ref, x_ref, out_ref, block_ref, sum_ref, o_ref, sems):
+    total = recv_ref.shape[0]
+    gk = coarse_ref.shape[1]
+    ck = turned_ref.shape[1]
+    cluster = lax.axis_index("wide").astype(jnp.int32)
+    block_ref[...] = jnp.zeros_like(block_ref)
+    for w in range(total // ck):
+        here = slice(w * ck, (w + 1) * ck)
+        block_ref[here, here] = recv_ref[here, rhs : rhs + ck]
+    forward = dot_parts(block_ref[...], recv_ref[:, :rhs], NN)
+    target = recv_ref[:, rhs + ck : rhs + ck + 1].astype(jnp.int32)
+    hot = (target == iota((total, gk), 1)).astype(F32).astype(BF16)
+    taken = dot_exact(coarse_ref[...], hot, NT)
+    sum_ref[...] = forward
+    mine = sum_ref[pl.ds(pl.multiple_of(cluster * ck, ck), ck), :]
+    corr = dot_parts(turned_ref[...], mine, NN) - dot_parts(taken, forward, NN)
+    write_out(corr.astype(BF16), sub, masked_ref, x_ref, out_ref, o_ref, sems)
+
+
+def last_kernel_plain(sub, corr_ref, masked_ref, x_ref, out_ref, o_ref, sems):
+    write_out(corr_ref[...].astype(BF16), sub, masked_ref, x_ref, out_ref, o_ref, sems)
 
 
 def per_device(duals, kernel, sub_counts, dual_sizes, cluster_factor, coarse_map, coarse_inverse):
@@ -253,10 +250,12 @@
     modes_first = stay(kernel.transpose(1, 0, 2))
     vectors = stay(duals)
     slabs = (count, rhs * sub, step)
+    small_enough = total * max(total, gk) <= 2**20
+    OUT = pltpu.VMEM if small_enough else jax.ShapeDtypeStruct
 
     send, inv = pl.pallas_call(
         functools.partial(first_kernel, rhs),
-        out_shape=(jax.ShapeDtypeStruct((total, lanes), F32), jax.ShapeDtypeStruct((ck, lanes), F32)),
+        out_shape=(jax.ShapeDtypeStruct((total, lanes), F32), OUT((ck, lanes), F32)),
         in_specs=[HBM] * 6,
         out_specs=(VMEM, VMEM),
         scratch_shapes=[
@@ -286,35 +285,38 @@
     for shift in range(1, members):
         picked = picked + lax.ppermute(part, "clus", [(i, (i + shift) % members) for i in range(members)])
     params = pltpu.CompilerParams(vmem_limit_bytes=LAST_LIMIT)
-    coarse, turned = pl.pallas_call(
-        functools.partial(middle_kernel, rhs, modes),
-        out_shape=(jax.ShapeDtypeStruct((padded, gk), F32), jax.ShapeDtypeStruct((padded, ck), F32)),
-        in_specs=[VMEM, VMEM],
-        out_specs=(VMEM, VMEM),
-        scratch_shapes=[pltpu.VMEM((ck, ck), F32)],
+    coarse, turned, masked, x = pl.pallas_call(
+        functools.partial(middle_kernel, rhs),
+        out_shape=(
+            OUT((padded, gk), F32),
+            OUT((padded, ck), F32),
+            OUT((rows, width), BF16),
+            OUT(slabs, BF16),
+        ),
+        in_specs=[VMEM, VMEM] + [HBM] * 4,
+        out_specs=(VMEM,) * 4,
+        scratch_shapes=[
+            pltpu.SMEM((1, 1), jnp.int32),
+            pltpu.SMEM((sub,), jnp.int32),
+            pltpu.VMEM((rows, width), BF16),
+            pltpu.VMEM((ck, ck), F32),
+            pltpu.SemaphoreType.DMA((count,)),
+            pltpu.SemaphoreType.DMA((3,)),
+        ],
         compiler_params=params,
-    )(inv, picked)
+    )(inv, picked, counts, sizes, modes_first, vectors)
 
     out_shape = jax.ShapeDtypeStruct(duals.shape, BF16)
-    scratch = [
-        pltpu.SMEM((1, 1), jnp.int32),
-        pltpu.SMEM((sub,), jnp.int32),
-        pltpu.VMEM((rows, width), BF16),
-        pltpu.VMEM(slabs, BF16),
-        pltpu.VMEM(slabs, BF16),
-        pltpu.SemaphoreType.DMA((count,)),
-        pltpu.SemaphoreType.DMA((count,)),
-        pltpu.SemaphoreType.DMA((3,)),
-    ]
-    if total * max(total, gk) <= 2**20:
+    scratch = [pltpu.VMEM(slabs, BF16), pltpu.SemaphoreType.DMA((count,))]
+    if small_enough:
         return pl.pallas_call(
-            functools.partial(last_kernel, rhs),
+            functools.partial(last_kernel, rhs, sub),
             out_shape=out_shape,
-            in_specs=[VMEM] * 3 + [HBM] * 4,
+            in_specs=[VMEM] * 5,
             out_specs=HBM,
             scratch_shapes=[pltpu.VMEM((total, total), F32), pltpu.VMEM((total, rhs), F32), *scratch],
             compiler_params=params,
-        )(recv.reshape(total, lanes), coarse, turned, counts, sizes, modes_first, vectors)
+        )(recv.reshape(total, lanes), coarse, turned, masked, x)
 
     blocks = recv.reshape(clusters, ck, lanes)
     forward = jnp.einsum("wam,wmr->war", blocks[:, :, rhs : rhs + ck], blocks[:, :, :rhs], precision=HI)
@@ -324,13 +326,13 @@
     mine = lax.dynamic_index_in_dim(forward, lax.axis_index("wide"), 0, keepdims=False)
     corr = jnp.dot(turned, mine, precision=HI) - jnp.dot(coarse, gsum, precision=HI)
     return pl.pallas_call(
-        last_kernel_plain,
+        functools.partial(last_kernel_plain, sub),
         out_shape=out_shape,
-        in_specs=[VMEM] + [HBM] * 4,
+        in_specs=[VMEM] * 3,
         out_specs=HBM,
         scratch_shapes=scratch,
         compiler_params=params,
-    )(corr, counts, sizes, modes_first, vectors)
+    )(corr, masked, x)
 
 
 def solution(mesh):

time: 23.5 us -> 23 us (0.979)
  Pallas kernels: 6.32 us -> 7.22 us
  local copies, waits for them, and re-layouts: 0.71 us -> 0.01 us
  waiting for transfers between devices: 7.38 us -> 6.8 us
    pallas_call x2, Pallas kernels: 3.31 us -> 4.2 us  [the longest x1 2.66 us: per_device(): pl.pallas_call(functools.partial(last_kernel, rhs, sub), out_shape=out_sh...]
    unnamed x6 -> x4, local copies, waits for them, and re-layouts: 0.71 us -> 0.01 us
    all_to_all x1, waiting for transfers between devices: 6.42 us -> 5.84 us  [per_device(): recv = lax.all_to_all(spread, ('wide', 'clus'), 0, 0)]
  transfers between devices with their start and end apart: 2 -> 2, of which waited for: 2 -> 2; matrix products, arithmetic and copies ran while one was open for 1% -> 1% of each run, Pallas kernels for 1% -> 7%
where the time goes in v4:
time: 23 us; the launch traced here: 22.7 us
  starting transfers between devices  7.64 us (33%)
  Pallas kernels  7.22 us (31%)
  waiting for transfers between devices  6.8 us (30%)
  between operations  0.75 us (3%)
  matrix products  0.23 us (1%)
    all_to_all x1, starting transfers between devices, per_device(): recv = lax.all_to_all(spread, ('wide', 'clus'), 0, 0)  7.33 us
    all_to_all x1, waiting for transfers between devices, per_device(): recv = lax.all_to_all(spread, ('wide', 'clus'), 0, 0)  5.84 us
    pallas_call x1, Pallas kernels, per_device(): pl.pallas_call(functools.partial(first_kernel, rhs), out_shape=(jax.Shape...  3.01 us
    pallas_call x1, Pallas kernels, per_device(): pl.pallas_call(functools.partial(last_kernel, rhs, sub), out_shape=out_sh...  2.66 us
    pallas_call x1, Pallas kernels, per_device(): pl.pallas_call(functools.partial(middle_kernel, rhs), out_shape=(OUT((pad...  1.55 us
    ppermute x1, waiting for transfers between devices, per_device(): lax.ppermute(part, 'clus', [(i, (i + shift) % members) for i in range(mem...  0.96 us
  transfers between devices with their start and end apart: 2, of which 2 were waited for; matrix products, arithmetic and copies ran while one was open for 1% of the time, Pallas kernels for 7%

profile of v4, /device:TPU:0, one launch (start us, length us, event | category | flops | bytes accessed | tf_op | source)
XLA Modules:
  0.0 22.7 jit_solution(17459062371009448830)
XLA Ops:
  0.0 0.0 copy-start
  0.0 0.0 copy-start.1
  0.7 3.0 %shard_map.73 = (f32[384,128]{1,0:T(8,128)}, f32[24,128]{1,0:T(8,128)S(1)}) custom-call(s32[1,1]{1,0:T(1,128)} %bitcast.8.counts_ref, s32[2]{0:T(128)} %sizes_ref.3, bf16[6,2,3840]{2,1,0:T(2,128)(2,1)} %bitcast.12, f32[24,24]{1,0:T(8,128)} %bitcast.15, s32[1,24]{1,0:T(1,128)} %map_ref.1, bf16[96,2,3840]{2,1,0:T(2,128)(2,1)} %duals_ref.3), custom_call_target="tpu_custom_call" | custom-call | tf_op jit(solution)/shard_map/pallas_call | solution.py:256
  3.7 7.3 %all-to-all-start = ((f32[32,12,1,128]{3,2,1,0:T(1,128)}), f32[32,12,1,128]{3,2,1,0:T(1,128)S(1)}, u32[]{:S(2)}, u32[]{:S(2)}) async-start(f32[32,12,1,128]{3,2,1,0:T(1,128)} %bitcast.14), calls=%async_computation | async-start | bytes 393216 | tf_op jit(solution)/shard_map/all_to_all | solution.py:279
  11.1 0.0 copy-done
  11.1 0.0 copy-done.1
  11.1 0.2 %fusion = f32[24,384]{1,0:T(8,128)S(1)} fusion(f32[192,384]{1,0:T(8,128)S(1)} %bitcast.10, s32[192]{0:T(256)S(1)} %iota_add_fusion, s32[24]{0:T(128)S(1)} %bitcast.16), kind=kOutput, calls=%fused_computation | convolution fusion | flops 21238272 | bytes 332640 | tf_op jit(solution)/shard_map/dot_general | solution.py:283
  11.3 0.3 %collective-permute-start = (f32[24,384]{1,0:T(8,128)S(1)}, f32[24,384]{1,0:T(8,128)S(1)}, u32[]{:S(2)}, u32[]{:S(2)}) collective-permute-start(f32[24,384]{1,0:T(8,128)S(1)} %fusion), channel_id=1, source_target_pairs={{0,1},{1,0},{2,3},{3,2},{4,5},{5,4},{6,7},{7,6},{8,9},{9,8},{10,11... | collective-permute-start | bytes 110600 | tf_op jit(solution)/shard_map/ppermute | solution.py:286
  11.6 1.0 %collective-permute-done = f32[24,384]{1,0:T(8,128)S(1)} collective-permute-done((f32[24,384]{1,0:T(8,128)S(1)}, f32[24,384]{1,0:T(8,128)S(1)}, u32[]{:S(2)}, u32[]{:S(2)}) %collective-permute-start) | collective-permute-done | bytes 36896 | tf_op jit(solution)/shard_map/ppermute | solution.py:286
  12.6 1.5 %shard_map.74 = (f32[16,384]{1,0:T(8,128)S(1)}, f32[16,24]{1,0:T(8,128)S(1)}, bf16[12,3840]{1,0:T(8,128)(2,1)S(1)}, bf16[5,192,768]{2,1,0:T(8,128)(2,1)S(1)}) custom-call(f32[24,128]{1,0:T(8,128)S(1)} %get-tuple-element.16.inv_ref, f32[24,384]{1,0:T(8,128)S(1)} %add.12.picked_ref, s32[1,1]{1,0:T(1,128)} %bitcast.9.counts_ref, s32[2]{0:T(128)} %sizes_ref.3, ...), custom_call_target="tpu_custom_call" | custom-call | tf_op jit(solution)/shard_map/pallas_call | solution.py:288
  14.2 5.8 %all-to-all-done = f32[32,12,1,128]{3,2,1,0:T(1,128)S(1)} async-done(((f32[32,12,1,128]{3,2,1,0:T(1,128)}), f32[32,12,1,128]{3,2,1,0:T(1,128)S(1)}, u32[]{:S(2)}, u32[]{:S(2)}) %all-to-all-start) | async-done | bytes 196640 | tf_op jit(solution)/shard_map/all_to_all | solution.py:279
  20.0 2.7 %shard_map.75 = bf16[96,2,3840]{2,1,0:T(2,128)(2,1)} custom-call(f32[384,128]{1,0:T(8,128)S(1)} %bitcast.11, f32[16,384]{1,0:T(8,128)S(1)} %get-tuple-element.19.coarse_ref, f32[16,24]{1,0:T(8,128)S(1)} %get-tuple-element.20.turned_ref, bf16[12,3840]{1,0:T(8,128)(2,1)S(1)} %get-tuple-element.21.masked_ref, bf16[5,192,768]{2,1,0:T(8,128)(2,1)S(1)} %get-tuple-element.22.x_ref), custom_call_target="tpu_custom_call" | custom-call | tf_op jit(solution)/shard_map/pallas_call | solution.py:312
  (2 shorter events, 0.0 us)
Async XLA Ops:
  0.0 11.1 %copy-start = (f32[384,192]{0,1:T(8,128)S(1)}, f32[384,192]{0,1:T(8,128)}, u32[]{:S(2)}) copy-start(f32[384,192]{0,1:T(8,128)} %param.13) | copy-start | bytes 884740
  0.0 11.1 %copy-start.1 = (s32[1,24]{1,0:T(1,128)S(1)}, s32[1,24]{1,0:T(1,128)}, u32[]{:S(2)}) copy-start(s32[1,24]{1,0:T(1,128)} %map_ref.1) | copy-start | bytes 292
  3.7 16.3 %all-to-all-start = ((f32[32,12,1,128]{3,2,1,0:T(1,128)}), f32[32,12,1,128]{3,2,1,0:T(1,128)S(1)}, u32[]{:S(2)}, u32[]{:S(2)}) async-start(f32[32,12,1,128]{3,2,1,0:T(1,128)} %bitcast.14), calls=%async_computation | async-start | bytes 393216 | tf_op jit(solution)/shard_map/all_to_all | solution.py:279
  11.3 1.3 %collective-permute-start = (f32[24,384]{1,0:T(8,128)S(1)}, f32[24,384]{1,0:T(8,128)S(1)}, u32[]{:S(2)}, u32[]{:S(2)}) collective-permute-start(f32[24,384]{1,0:T(8,128)S(1)} %fusion), channel_id=1, source_target_pairs={{0,1},{1,0},{2,3},{3,2},{4,5},{5,4},{6,7},{7,6},{8,9},{9,8},{10,11... | collective-permute-start | bytes 110600 | tf_op jit(solution)/shard_map/ppermute | solution.py:286

commit v5 on v4

--- a/solution.py
+++ b/solution.py
@@ -17,6 +17,7 @@
 HBM = pl.BlockSpec(memory_space=pltpu.HBM)
 FIRST_LIMIT = 60 * 2**20
 LAST_LIMIT = 20 * 2**20
+AHEAD = 3
 
 
 def iota(shape, dim):
@@ -71,12 +72,14 @@
 
 
 def slab_copies(whole_ref, slabs_ref, sems, back=False):
-    count, rows, step = slabs_ref.shape
+    count, _, step = slabs_ref.shape
+    rows = whole_ref.shape[0] * whole_ref.shape[1]
     flat = whole_ref.reshape(rows, count * step)
 
     def copy(n):
         part = flat.at[:, pl.ds(n * step, step)]
-        ends = (slabs_ref.at[n], part) if back else (part, slabs_ref.at[n])
+        slab = slabs_ref.at[n, pl.ds(0, rows)]
+        ends = (slab, part) if back else (part, slab)
         return pltpu.make_async_copy(*ends, sems.at[n])
 
     return copy
@@ -161,12 +164,13 @@
 
 
 def middle_kernel(rhs, inv_ref, picked_ref, counts_ref, sizes_ref, kernel_ref, duals_ref,
-                  coarse_ref, turned_ref, masked_ref, x_ref,
+                  coarse_ref, turned_ref, x_ref,
                   count_s, size_s, raw_ref, turn_ref, sems, small_sems):
     modes, sub, width = kernel_ref.shape
     rows = modes * sub
     ck = picked_ref.shape[0]
-    count = x_ref.shape[0]
+    count, deep, step = x_ref.shape
+    flat = duals_ref.shape[0] * sub
     copy = slab_copies(duals_ref, x_ref, sems)
     small = [
         pltpu.make_async_copy(src, dst, small_sems.at[n])
@@ -186,48 +190,75 @@
     coarse_ref[...] = lax.dot_general(turned_ref[...], picked_ref[...], NN, precision=HI, preferred_element_type=F32)
     for one in small:
         one.wait()
-    masked_ref[...] = mask_kernel(raw_ref, count_s, size_s, sub)
+    masked = mask_kernel(raw_ref, count_s, size_s, sub)
+    for n in range(count):
+        x_ref[n, flat:, :] = jnp.zeros((deep - flat, step), BF16)
+        x_ref[n, flat : flat + rows, :] = masked[:, n * step : (n + 1) * step]
     for n in range(count):
         copy(n).wait()
 
 
-def write_out(corr, sub, masked_ref, x_ref, out_ref, o_ref, sems):
-    rows = masked_ref.shape[0]
-    count, flat, step = x_ref.shape
-    rhs = flat // sub
+def write_out(corr, sub, x_ref, out_ref, corr_ref, o_ref, sems):
+    flat, rhs = o_ref.shape[1], corr_ref.shape[1]
+    count, deep, step = x_ref.shape
     copy = slab_copies(out_ref, o_ref, sems, back=True)
-    wide = dot(rows_of_slots(sub, rhs, rhs), corr, NT)
-    same = iota(wide.shape, 0) % sub == iota(wide.shape, 1) % sub
-    wide = jnp.where(same, wide, 0.0)[:, :rows].astype(BF16)
-    for n in range(count):
-        delta = dot(wide, masked_ref[:, n * step : (n + 1) * step], NN)
-        o_ref[n] = (x_ref[n].astype(F32) - delta).astype(BF16)
-        copy(n).start()
+    corr_ref[:flat, :] = jnp.zeros((flat, rhs), BF16)
+    corr_ref[flat:, :] = -corr
+    wide = dot(rows_of_slots(sub, rhs, rhs), corr_ref[...], NT)
+    row, col = iota(wide.shape, 0), iota(wide.shape, 1)
+    same = (col >= flat) & (row % sub == col % sub)
+    left = jnp.where(same, wide, (row == col).astype(F32)).astype(BF16)
+    tile = 2 * LANES if step % (2 * LANES) == 0 else LANES
+    tiles = [(n, slice(c, c + tile)) for n in range(count) for c in range(0, step, tile)]
+    waiting = []
+    for n, cols in [*tiles, *[(None, None)] * AHEAD]:
+        if n is not None:
+            waiting.append((n, cols, dot(left, x_ref[n, :, cols], NN)))
+        if len(waiting) > AHEAD or n is None and waiting:
+            done, where, value = waiting.pop(0)
+            o_ref[done, :, where] = value.astype(BF16)
+            if where.stop == step:
+                copy(done).start()
     for n in range(count):
         copy(n).wait()
 
 
-def last_kernel(rhs, sub, recv_ref, coarse_ref, turned_ref, masked_ref, x_ref, out_ref, block_ref, sum_ref, o_ref, sems):
+def block_product(recv_ref, rhs, ck, block_ref):
+    total = recv_ref.shape[0]
+    block_ref[...] = jnp.zeros_like(block_ref)
+    for w in range(total // ck):
+        here = slice(w * ck, (w + 1) * ck)
+        block_ref[here, here] = recv_ref[here, rhs : rhs + ck]
+    spans = []
+    for start in range(0, total, LANES):
+        stop = min(start + LANES, total)
+        low = start // ck * ck // 16 * 16
+        high = min(up(up(stop, ck), 16), total)
+        spans.append((low, high, dot_parts(block_ref[low:high, start:stop], recv_ref[start:stop, :rhs], NN)))
+    return spans
+
+
+def last_kernel(rhs, sub, recv_ref, coarse_ref, turned_ref, x_ref, out_ref, block_ref, sum_ref, corr_ref, o_ref, sems):
     total = recv_ref.shape[0]
     gk = coarse_ref.shape[1]
     ck = turned_ref.shape[1]
     cluster = lax.axis_index("wide").astype(jnp.int32)
-    block_ref[...] = jnp.zeros_like(block_ref)
-    for w in range(total // ck):
-        here = slice(w * ck, (w + 1) * ck)
-        block_ref[here, here] = recv_ref[here, rhs : rhs + ck]
-    forward = dot_parts(block_ref[...], recv_ref[:, :rhs], NN)
+    done = 0
+    for low, high, part in block_product(recv_ref, rhs, ck, block_ref):
+        if low < done:
+            sum_ref[low:done, :] += part[: done - low]
+        sum_ref[done:high, :] = part[done - low :]
+        done = high
     target = recv_ref[:, rhs + ck : rhs + ck + 1].astype(jnp.int32)
     hot = (target == iota((total, gk), 1)).astype(F32).astype(BF16)
     taken = dot_exact(coarse_ref[...], hot, NT)
-    sum_ref[...] = forward
     mine = sum_ref[pl.ds(pl.multiple_of(cluster * ck, ck), ck), :]
-    corr = dot_parts(turned_ref[...], mine, NN) - dot_parts(taken, forward, NN)
-    write_out(corr.astype(BF16), sub, masked_ref, x_ref, out_ref, o_ref, sems)
-
-
-def last_kernel_plain(sub, corr_ref, masked_ref, x_ref, out_ref, o_ref, sems):
-    write_out(corr_ref[...].astype(BF16), sub, masked_ref, x_ref, out_ref, o_ref, sems)
+    corr = dot_parts(turned_ref[...], mine, NN) - dot_parts(taken, sum_ref[...], NN)
+    write_out(corr.astype(BF16), sub, x_ref, out_ref, corr_ref, o_ref, sems)
+
+
+def last_kernel_plain(sub, given_ref, x_ref, out_ref, corr_ref, o_ref, sems):
+    write_out(given_ref[...].astype(BF16), sub, x_ref, out_ref, corr_ref, o_ref, sems)
 
 
 def per_device(duals, kernel, sub_counts, dual_sizes, cluster_factor, coarse_map, coarse_inverse):
@@ -250,6 +281,7 @@
     modes_first = stay(kernel.transpose(1, 0, 2))
     vectors = stay(duals)
     slabs = (count, rhs * sub, step)
+    deeper = (count, rhs * sub + padded, step)
     small_enough = total * max(total, gk) <= 2**20
     OUT = pltpu.VMEM if small_enough else jax.ShapeDtypeStruct
 
@@ -285,16 +317,15 @@
     for shift in range(1, members):
         picked = picked + lax.ppermute(part, "clus", [(i, (i + shift) % members) for i in range(members)])
     params = pltpu.CompilerParams(vmem_limit_bytes=LAST_LIMIT)
-    coarse, turned, masked, x = pl.pallas_call(
+    coarse, turned, x = pl.pallas_call(
         functools.partial(middle_kernel, rhs),
         out_shape=(
             OUT((padded, gk), F32),
             OUT((padded, ck), F32),
-            OUT((rows, width), BF16),
-            OUT(slabs, BF16),
+            OUT(deeper, BF16),
         ),
         in_specs=[VMEM, VMEM] + [HBM] * 4,
-        out_specs=(VMEM,) * 4,
+        out_specs=(VMEM,) * 3,
         scratch_shapes=[
             pltpu.SMEM((1, 1), jnp.int32),
             pltpu.SMEM((sub,), jnp.int32),
@@ -307,16 +338,20 @@
     )(inv, picked, counts, sizes, modes_first, vectors)
 
     out_shape = jax.ShapeDtypeStruct(duals.shape, BF16)
-    scratch = [pltpu.VMEM(slabs, BF16), pltpu.SemaphoreType.DMA((count,))]
+    scratch = [
+        pltpu.VMEM((rhs * sub + padded, rhs), BF16),
+        pltpu.VMEM(slabs, BF16),
+        pltpu.SemaphoreType.DMA((count,)),
+    ]
     if small_enough:
         return pl.pallas_call(
             functools.partial(last_kernel, rhs, sub),
             out_shape=out_shape,
-            in_specs=[VMEM] * 5,
+            in_specs=[VMEM] * 4,
             out_specs=HBM,
             scratch_shapes=[pltpu.VMEM((total, total), F32), pltpu.VMEM((total, rhs), F32), *scratch],
             compiler_params=params,
-        )(recv.reshape(total, lanes), coarse, turned, masked, x)
+        )(recv.reshape(total, lanes), coarse, turned, x)
 
     blocks = recv.reshape(clusters, ck, lanes)
     forward = jnp.einsum("wam,wmr->war", blocks[:, :, rhs : rhs + ck], blocks[:, :, :rhs], precision=HI)
@@ -328,11 +363,11 @@
     return pl.pallas_call(
         functools.partial(last_kernel_plain, sub),
         out_shape=out_shape,
-        in_specs=[VMEM] * 3,
+        in_specs=[VMEM] * 2,
         out_specs=HBM,
         scratch_shapes=scratch,
         compiler_params=params,
-    )(corr, masked, x)
+    )(corr, x)
 
 
 def solution(mesh):

time: 23 us -> 22.6 us (0.983)
  Pallas kernels: 7.22 us -> 6.79 us
    pallas_call x1, Pallas kernels: 2.66 us -> 2.23 us  [per_device(): pl.pallas_call(functools.partial(last_kernel, rhs, sub), out_shape=out_sh...]
where the time goes in v5:
time: 22.6 us; the launch traced here: 22.2 us
  starting transfers between devices  7.64 us (34%)
  waiting for transfers between devices  6.8 us (30%)
  Pallas kernels  6.79 us (30%)
  between operations  0.75 us (3%)
  matrix products  0.23 us (1%)
    all_to_all x1, starting transfers between devices, per_device(): recv = lax.all_to_all(spread, ('wide', 'clus'), 0, 0)  7.33 us
    all_to_all x1, waiting for transfers between devices, per_device(): recv = lax.all_to_all(spread, ('wide', 'clus'), 0, 0)  5.84 us
    pallas_call x1, Pallas kernels, per_device(): pl.pallas_call(functools.partial(first_kernel, rhs), out_shape=(jax.Shape...  3.01 us
    pallas_call x1, Pallas kernels, per_device(): pl.pallas_call(functools.partial(last_kernel, rhs, sub), out_shape=out_sh...  2.23 us
    pallas_call x1, Pallas kernels, per_device(): pl.pallas_call(functools.partial(middle_kernel, rhs), out_shape=(OUT((pad...  1.55 us
    ppermute x1, waiting for transfers between devices, per_device(): lax.ppermute(part, 'clus', [(i, (i + shift) % members) for i in range(mem...  0.96 us
  transfers between devices with their start and end apart: 2, of which 2 were waited for; matrix products, arithmetic and copies ran while one was open for 1% of the time, Pallas kernels for 7%

profile of v5, /device:TPU:0, one launch (start us, length us, event | category | flops | bytes accessed | tf_op | source)
XLA Modules:
  0.0 22.2 jit_solution(6677996436693092422)
XLA Ops:
  0.0 0.0 copy-start
  0.0 0.0 copy-start.1
  0.7 3.0 %shard_map.73 = (f32[384,128]{1,0:T(8,128)}, f32[24,128]{1,0:T(8,128)S(1)}) custom-call(s32[1,1]{1,0:T(1,128)} %bitcast.8.counts_ref, s32[2]{0:T(128)} %sizes_ref.3, bf16[6,2,3840]{2,1,0:T(2,128)(2,1)} %bitcast.12, f32[24,24]{1,0:T(8,128)} %bitcast.15, s32[1,24]{1,0:T(1,128)} %map_ref.1, bf16[96,2,3840]{2,1,0:T(2,128)(2,1)} %duals_ref.3), custom_call_target="tpu_custom_call" | custom-call | tf_op jit(solution)/shard_map/pallas_call | solution.py:288
  3.7 7.3 %all-to-all-start = ((f32[32,12,1,128]{3,2,1,0:T(1,128)}), f32[32,12,1,128]{3,2,1,0:T(1,128)S(1)}, u32[]{:S(2)}, u32[]{:S(2)}) async-start(f32[32,12,1,128]{3,2,1,0:T(1,128)} %bitcast.14), calls=%async_computation | async-start | bytes 393216 | tf_op jit(solution)/shard_map/all_to_all | solution.py:311
  11.1 0.0 copy-done
  11.1 0.0 copy-done.1
  11.1 0.2 %fusion = f32[24,384]{1,0:T(8,128)S(1)} fusion(f32[192,384]{1,0:T(8,128)S(1)} %bitcast.10, s32[192]{0:T(256)S(1)} %iota_add_fusion, s32[24]{0:T(128)S(1)} %bitcast.16), kind=kOutput, calls=%fused_computation | convolution fusion | flops 21238272 | bytes 332640 | tf_op jit(solution)/shard_map/dot_general | solution.py:315
  11.3 0.3 %collective-permute-start = (f32[24,384]{1,0:T(8,128)S(1)}, f32[24,384]{1,0:T(8,128)S(1)}, u32[]{:S(2)}, u32[]{:S(2)}) collective-permute-start(f32[24,384]{1,0:T(8,128)S(1)} %fusion), channel_id=1, source_target_pairs={{0,1},{1,0},{2,3},{3,2},{4,5},{5,4},{6,7},{7,6},{8,9},{9,8},{10,11... | collective-permute-start | bytes 110600 | tf_op jit(solution)/shard_map/ppermute | solution.py:318
  11.6 1.0 %collective-permute-done = f32[24,384]{1,0:T(8,128)S(1)} collective-permute-done((f32[24,384]{1,0:T(8,128)S(1)}, f32[24,384]{1,0:T(8,128)S(1)}, u32[]{:S(2)}, u32[]{:S(2)}) %collective-permute-start) | collective-permute-done | bytes 36896 | tf_op jit(solution)/shard_map/ppermute | solution.py:318
  12.6 1.5 %shard_map.74 = (f32[16,384]{1,0:T(8,128)S(1)}, f32[16,24]{1,0:T(8,128)S(1)}, bf16[5,208,768]{2,1,0:T(8,128)(2,1)S(1)}) custom-call(f32[24,128]{1,0:T(8,128)S(1)} %get-tuple-element.15.inv_ref, f32[24,384]{1,0:T(8,128)S(1)} %add.12.picked_ref, s32[1,1]{1,0:T(1,128)} %bitcast.9.counts_ref, s32[2]{0:T(128)} %sizes_ref.3, bf16[6,2,3840]{2,1,0:T(2,128)(2,1)} %bitcast.13, ...), custom_call_target="tpu_custom_call" | custom-call | tf_op jit(solution)/shard_map/pallas_call | solution.py:320
  14.2 5.8 %all-to-all-done = f32[32,12,1,128]{3,2,1,0:T(1,128)S(1)} async-done(((f32[32,12,1,128]{3,2,1,0:T(1,128)}), f32[32,12,1,128]{3,2,1,0:T(1,128)S(1)}, u32[]{:S(2)}, u32[]{:S(2)}) %all-to-all-start) | async-done | bytes 196640 | tf_op jit(solution)/shard_map/all_to_all | solution.py:311
  20.0 2.2 %shard_map.75 = bf16[96,2,3840]{2,1,0:T(2,128)(2,1)} custom-call(f32[384,128]{1,0:T(8,128)S(1)} %bitcast.11, f32[16,384]{1,0:T(8,128)S(1)} %get-tuple-element.18.coarse_ref, f32[16,24]{1,0:T(8,128)S(1)} %get-tuple-element.19.turned_ref, bf16[5,208,768]{2,1,0:T(8,128)(2,1)S(1)} %get-tuple-element.20.x_ref), custom_call_target="tpu_custom_call" | custom-call | tf_op jit(solution)/shard_map/pallas_call | solution.py:347
  (2 shorter events, 0.0 us)
Async XLA Ops:
  0.0 11.1 %copy-start = (f32[384,192]{0,1:T(8,128)S(1)}, f32[384,192]{0,1:T(8,128)}, u32[]{:S(2)}) copy-start(f32[384,192]{0,1:T(8,128)} %param.13) | copy-start | bytes 884740
  0.0 11.1 %copy-start.1 = (s32[1,24]{1,0:T(1,128)S(1)}, s32[1,24]{1,0:T(1,128)}, u32[]{:S(2)}) copy-start(s32[1,24]{1,0:T(1,128)} %map_ref.1) | copy-start | bytes 292
  3.7 16.3 %all-to-all-start = ((f32[32,12,1,128]{3,2,1,0:T(1,128)}), f32[32,12,1,128]{3,2,1,0:T(1,128)S(1)}, u32[]{:S(2)}, u32[]{:S(2)}) async-start(f32[32,12,1,128]{3,2,1,0:T(1,128)} %bitcast.14), calls=%async_computation | async-start | bytes 393216 | tf_op jit(solution)/shard_map/all_to_all | solution.py:311
  11.3 1.3 %collective-permute-start = (f32[24,384]{1,0:T(8,128)S(1)}, f32[24,384]{1,0:T(8,128)S(1)}, u32[]{:S(2)}, u32[]{:S(2)}) collective-permute-start(f32[24,384]{1,0:T(8,128)S(1)} %fusion), channel_id=1, source_target_pairs={{0,1},{1,0},{2,3},{3,2},{4,5},{5,4},{6,7},{7,6},{8,9},{9,8},{10,11... | collective-permute-start | bytes 110600 | tf_op jit(solution)/shard_map/ppermute | solution.py:318

commit v6 on v5

--- a/solution.py
+++ b/solution.py
@@ -17,7 +17,7 @@
 HBM = pl.BlockSpec(memory_space=pltpu.HBM)
 FIRST_LIMIT = 60 * 2**20
 LAST_LIMIT = 20 * 2**20
-AHEAD = 3
+AHEAD = 8
 
 
 def iota(shape, dim):
@@ -144,10 +144,14 @@
         one.wait()
     masked = mask_kernel(raw_ref, count_s, size_s, sub)
     acc_ref[...] = jnp.zeros_like(acc_ref)
-    total = jnp.zeros((rows, rhs * sub), F32)
+    cut = up(rhs * sub // 2, 16)
+    halves = [(0, cut), (cut, rhs * sub)]
+    sums = [jnp.zeros((rows, stop - start), F32) for start, stop in halves]
     for n in range(count):
         copy(n).wait()
-        total = total + dot(masked[:, n * step : (n + 1) * step], x_ref[n], NT)
+        weight = masked[:, n * step : (n + 1) * step]
+        sums = [part + dot(weight, x_ref[n, start:stop, :], NT) for part, (start, stop) in zip(sums, halves)]
+    total = jnp.concatenate(sums, axis=1)
     same = iota((rows, rhs * sub), 0) % sub == iota((rows, rhs * sub), 1) % sub
     acc_ref[:rows, :] = jnp.where(same, total, 0.0)
     mixed = dot_exact(acc_ref[...], rows_of_slots(sub, rhs, lanes), NN)

time: 22.6 us -> 22.1 us (0.978)
  Pallas kernels: 6.79 us -> 6.37 us
    pallas_call x1, Pallas kernels: 3.01 us -> 2.72 us  [per_device(): pl.pallas_call(functools.partial(first_kernel, rhs), out_shape=(jax.Shape...]
where the time goes in v6:
time: 22.1 us; the launch traced here: 21.8 us
  starting transfers between devices  7.64 us (35%)
  waiting for transfers between devices  6.8 us (31%)
  Pallas kernels  6.37 us (29%)
  between operations  0.75 us (3%)
  matrix products  0.23 us (1%)
    all_to_all x1, starting transfers between devices, per_device(): recv = lax.all_to_all(spread, ('wide', 'clus'), 0, 0)  7.33 us
    all_to_all x1, waiting for transfers between devices, per_device(): recv = lax.all_to_all(spread, ('wide', 'clus'), 0, 0)  5.84 us
    pallas_call x1, Pallas kernels, per_device(): pl.pallas_call(functools.partial(first_kernel, rhs), out_shape=(jax.Shape...  2.72 us
    pallas_call x1, Pallas kernels, per_device(): pl.pallas_call(functools.partial(last_kernel, rhs, sub), out_shape=out_sh...  2.11 us
    pallas_call x1, Pallas kernels, per_device(): pl.pallas_call(functools.partial(middle_kernel, rhs), out_shape=(OUT((pad...  1.55 us
    ppermute x1, waiting for transfers between devices, per_device(): lax.ppermute(part, 'clus', [(i, (i + shift) % members) for i in range(mem...  0.96 us
  transfers between devices with their start and end apart: 2, of which 2 were waited for; matrix products, arithmetic and copies ran while one was open for 1% of the time, Pallas kernels for 7%

profile of v6, /device:TPU:0, one launch (start us, length us, event | category | flops | bytes accessed | tf_op | source)
XLA Modules:
  0.0 21.8 jit_solution(2624745671541877258)
XLA Ops:
  0.0 0.0 copy-start
  0.0 0.0 copy-start.1
  0.7 2.7 %shard_map.73 = (f32[384,128]{1,0:T(8,128)}, f32[24,128]{1,0:T(8,128)S(1)}) custom-call(s32[1,1]{1,0:T(1,128)} %bitcast.8.counts_ref, s32[2]{0:T(128)} %sizes_ref.3, bf16[6,2,3840]{2,1,0:T(2,128)(2,1)} %bitcast.12, f32[24,24]{1,0:T(8,128)} %bitcast.15, s32[1,24]{1,0:T(1,128)} %map_ref.1, bf16[96,2,3840]{2,1,0:T(2,128)(2,1)} %duals_ref.3), custom_call_target="tpu_custom_call" | custom-call | tf_op jit(solution)/shard_map/pallas_call | solution.py:292
  3.4 7.3 %all-to-all-start = ((f32[32,12,1,128]{3,2,1,0:T(1,128)}), f32[32,12,1,128]{3,2,1,0:T(1,128)S(1)}, u32[]{:S(2)}, u32[]{:S(2)}) async-start(f32[32,12,1,128]{3,2,1,0:T(1,128)} %bitcast.14), calls=%async_computation | async-start | bytes 393216 | tf_op jit(solution)/shard_map/all_to_all | solution.py:315
  10.8 0.0 copy-done
  10.8 0.0 copy-done.1
  10.8 0.2 %fusion = f32[24,384]{1,0:T(8,128)S(1)} fusion(f32[192,384]{1,0:T(8,128)S(1)} %bitcast.10, s32[192]{0:T(256)S(1)} %iota_add_fusion, s32[24]{0:T(128)S(1)} %bitcast.16), kind=kOutput, calls=%fused_computation | convolution fusion | flops 21238272 | bytes 332640 | tf_op jit(solution)/shard_map/dot_general | solution.py:319
  11.0 0.3 %collective-permute-start = (f32[24,384]{1,0:T(8,128)S(1)}, f32[24,384]{1,0:T(8,128)S(1)}, u32[]{:S(2)}, u32[]{:S(2)}) collective-permute-start(f32[24,384]{1,0:T(8,128)S(1)} %fusion), channel_id=1, source_target_pairs={{0,1},{1,0},{2,3},{3,2},{4,5},{5,4},{6,7},{7,6},{8,9},{9,8},{10,11... | collective-permute-start | bytes 110600 | tf_op jit(solution)/shard_map/ppermute | solution.py:322
  11.3 1.0 %collective-permute-done = f32[24,384]{1,0:T(8,128)S(1)} collective-permute-done((f32[24,384]{1,0:T(8,128)S(1)}, f32[24,384]{1,0:T(8,128)S(1)}, u32[]{:S(2)}, u32[]{:S(2)}) %collective-permute-start) | collective-permute-done | bytes 36896 | tf_op jit(solution)/shard_map/ppermute | solution.py:322
  12.3 1.5 %shard_map.74 = (f32[16,384]{1,0:T(8,128)S(1)}, f32[16,24]{1,0:T(8,128)S(1)}, bf16[5,208,768]{2,1,0:T(8,128)(2,1)S(1)}) custom-call(f32[24,128]{1,0:T(8,128)S(1)} %get-tuple-element.15.inv_ref, f32[24,384]{1,0:T(8,128)S(1)} %add.12.picked_ref, s32[1,1]{1,0:T(1,128)} %bitcast.9.counts_ref, s32[2]{0:T(128)} %sizes_ref.3, bf16[6,2,3840]{2,1,0:T(2,128)(2,1)} %bitcast.13, ...), custom_call_target="tpu_custom_call" | custom-call | tf_op jit(solution)/shard_map/pallas_call | solution.py:324
  13.9 5.8 %all-to-all-done = f32[32,12,1,128]{3,2,1,0:T(1,128)S(1)} async-done(((f32[32,12,1,128]{3,2,1,0:T(1,128)}), f32[32,12,1,128]{3,2,1,0:T(1,128)S(1)}, u32[]{:S(2)}, u32[]{:S(2)}) %all-to-all-start) | async-done | bytes 196640 | tf_op jit(solution)/shard_map/all_to_all | solution.py:315
  19.7 2.1 %shard_map.75 = bf16[96,2,3840]{2,1,0:T(2,128)(2,1)} custom-call(f32[384,128]{1,0:T(8,128)S(1)} %bitcast.11, f32[16,384]{1,0:T(8,128)S(1)} %get-tuple-element.18.coarse_ref, f32[16,24]{1,0:T(8,128)S(1)} %get-tuple-element.19.turned_ref, bf16[5,208,768]{2,1,0:T(8,128)(2,1)S(1)} %get-tuple-element.20.x_ref), custom_call_target="tpu_custom_call" | custom-call | tf_op jit(solution)/shard_map/pallas_call | solution.py:351
  (2 shorter events, 0.0 us)
Async XLA Ops:
  0.0 10.8 %copy-start = (f32[384,192]{0,1:T(8,128)S(1)}, f32[384,192]{0,1:T(8,128)}, u32[]{:S(2)}) copy-start(f32[384,192]{0,1:T(8,128)} %param.13) | copy-start | bytes 884740
  0.0 10.8 %copy-start.1 = (s32[1,24]{1,0:T(1,128)S(1)}, s32[1,24]{1,0:T(1,128)}, u32[]{:S(2)}) copy-start(s32[1,24]{1,0:T(1,128)} %map_ref.1) | copy-start | bytes 292
  3.4 16.3 %all-to-all-start = ((f32[32,12,1,128]{3,2,1,0:T(1,128)}), f32[32,12,1,128]{3,2,1,0:T(1,128)S(1)}, u32[]{:S(2)}, u32[]{:S(2)}) async-start(f32[32,12,1,128]{3,2,1,0:T(1,128)} %bitcast.14), calls=%async_computation | async-start | bytes 393216 | tf_op jit(solution)/shard_map/all_to_all | solution.py:315
  11.0 1.3 %collective-permute-start = (f32[24,384]{1,0:T(8,128)S(1)}, f32[24,384]{1,0:T(8,128)S(1)}, u32[]{:S(2)}, u32[]{:S(2)}) collective-permute-start(f32[24,384]{1,0:T(8,128)S(1)} %fusion), channel_id=1, source_target_pairs={{0,1},{1,0},{2,3},{3,2},{4,5},{5,4},{6,7},{7,6},{8,9},{9,8},{10,11... | collective-permute-start | bytes 110600 | tf_op jit(solution)/shard_map/ppermute | solution.py:322

commit v7 on v6

--- a/solution.py
+++ b/solution.py
@@ -67,20 +67,22 @@
     return 1
 
 
+def tile_of(step):
+    return 2 * LANES if step % (2 * LANES) == 0 else LANES
+
+
 def rows_of_slots(sub, rhs, lanes):
     return (iota((rhs * sub, lanes), 0) // sub == iota((rhs * sub, lanes), 1)).astype(F32).astype(BF16)
 
 
-def slab_copies(whole_ref, slabs_ref, sems, back=False):
+def slab_copies(whole_ref, slabs_ref, sems):
     count, _, step = slabs_ref.shape
     rows = whole_ref.shape[0] * whole_ref.shape[1]
     flat = whole_ref.reshape(rows, count * step)
 
     def copy(n):
         part = flat.at[:, pl.ds(n * step, step)]
-        slab = slabs_ref.at[n, pl.ds(0, rows)]
-        ends = (slab, part) if back else (part, slab)
-        return pltpu.make_async_copy(*ends, sems.at[n])
+        return pltpu.make_async_copy(part, slabs_ref.at[n, pl.ds(0, rows)], sems.at[n])
 
     return copy
 
@@ -205,14 +207,23 @@
 def write_out(corr, sub, x_ref, out_ref, corr_ref, o_ref, sems):
     flat, rhs = o_ref.shape[1], corr_ref.shape[1]
     count, deep, step = x_ref.shape
-    copy = slab_copies(out_ref, o_ref, sems, back=True)
-    corr_ref[:flat, :] = jnp.zeros((flat, rhs), BF16)
-    corr_ref[flat:, :] = -corr
+    base = flat // LANES * LANES
+    corr_ref[: flat - base, :] = jnp.zeros((flat - base, rhs), BF16)
+    corr_ref[flat - base :, :] = -corr
     wide = dot(rows_of_slots(sub, rhs, rhs), corr_ref[...], NT)
-    row, col = iota(wide.shape, 0), iota(wide.shape, 1)
+    row, col = iota(wide.shape, 0), iota(wide.shape, 1) + base
     same = (col >= flat) & (row % sub == col % sub)
     left = jnp.where(same, wide, (row == col).astype(F32)).astype(BF16)
-    tile = 2 * LANES if step % (2 * LANES) == 0 else LANES
+    if base:
+        eye = (iota((flat, base), 0) == iota((flat, base), 1)).astype(F32).astype(BF16)
+        left = jnp.concatenate([eye, left], axis=1)
+    tile = tile_of(step)
+    out_flat = out_ref.reshape(flat, count * step)
+
+    def copy(n, cols):
+        part = out_flat.at[:, pl.ds(n * step + cols.start, tile)]
+        return pltpu.make_async_copy(o_ref.at[n, :, cols], part, sems.at[n, cols.start // tile])
+
     tiles = [(n, slice(c, c + tile)) for n in range(count) for c in range(0, step, tile)]
     waiting = []
     for n, cols in [*tiles, *[(None, None)] * AHEAD]:
@@ -221,10 +232,9 @@
         if len(waiting) > AHEAD or n is None and waiting:
             done, where, value = waiting.pop(0)
             o_ref[done, :, where] = value.astype(BF16)
-            if where.stop == step:
-                copy(done).start()
-    for n in range(count):
-        copy(n).wait()
+            copy(done, where).start()
+    for n, cols in tiles:
+        copy(n, cols).wait()
 
 
 def block_product(recv_ref, rhs, ck, block_ref):
@@ -343,9 +353,9 @@
 
     out_shape = jax.ShapeDtypeStruct(duals.shape, BF16)
     scratch = [
-        pltpu.VMEM((rhs * sub + padded, rhs), BF16),
+        pltpu.VMEM((rhs * sub % LANES + padded, rhs), BF16),
         pltpu.VMEM(slabs, BF16),
-        pltpu.SemaphoreType.DMA((count,)),
+        pltpu.SemaphoreType.DMA((count, step // tile_of(step))),
     ]
     if small_enough:
         return pl.pallas_call(

time: 22.1 us -> 22.1 us (level)
  no operation moved by 1% of the time
where the time goes in v7:
time: 22.1 us; the launch traced here: 21.8 us
  starting transfers between devices  7.64 us (35%)
  waiting for transfers between devices  6.8 us (31%)
  Pallas kernels  6.34 us (29%)
  between operations  0.75 us (3%)
  matrix products  0.23 us (1%)
    all_to_all x1, starting transfers between devices, per_device(): recv = lax.all_to_all(spread, ('wide', 'clus'), 0, 0)  7.33 us
    all_to_all x1, waiting for transfers between devices, per_device(): recv = lax.all_to_all(spread, ('wide', 'clus'), 0, 0)  5.84 us
    pallas_call x1, Pallas kernels, per_device(): pl.pallas_call(functools.partial(first_kernel, rhs), out_shape=(jax.Shape...  2.72 us
    pallas_call x1, Pallas kernels, per_device(): pl.pallas_call(functools.partial(last_kernel, rhs, sub), out_shape=out_sh...  2.08 us
    pallas_call x1, Pallas kernels, per_device(): pl.pallas_call(functools.partial(middle_kernel, rhs), out_shape=(OUT((pad...  1.55 us
    ppermute x1, waiting for transfers between devices, per_device(): lax.ppermute(part, 'clus', [(i, (i + shift) % members) for i in range(mem...  0.96 us
  transfers between devices with their start and end apart: 2, of which 2 were waited for; matrix products, arithmetic and copies ran while one was open for 1% of the time, Pallas kernels for 7%

profile of v7, /device:TPU:0, one launch (start us, length us, event | category | flops | bytes accessed | tf_op | source)
XLA Modules:
  0.0 21.8 jit_solution(8390595761153893858)
XLA Ops:
  0.0 0.0 copy-start
  0.0 0.0 copy-start.1
  0.7 2.7 %shard_map.73 = (f32[384,128]{1,0:T(8,128)}, f32[24,128]{1,0:T(8,128)S(1)}) custom-call(s32[1,1]{1,0:T(1,128)} %bitcast.8.counts_ref, s32[2]{0:T(128)} %sizes_ref.3, bf16[6,2,3840]{2,1,0:T(2,128)(2,1)} %bitcast.12, f32[24,24]{1,0:T(8,128)} %bitcast.15, s32[1,24]{1,0:T(1,128)} %map_ref.1, bf16[96,2,3840]{2,1,0:T(2,128)(2,1)} %duals_ref.3), custom_call_target="tpu_custom_call" | custom-call | tf_op jit(solution)/shard_map/pallas_call | solution.py:302
  3.4 7.3 %all-to-all-start = ((f32[32,12,1,128]{3,2,1,0:T(1,128)}), f32[32,12,1,128]{3,2,1,0:T(1,128)S(1)}, u32[]{:S(2)}, u32[]{:S(2)}) async-start(f32[32,12,1,128]{3,2,1,0:T(1,128)} %bitcast.14), calls=%async_computation | async-start | bytes 393216 | tf_op jit(solution)/shard_map/all_to_all | solution.py:325
  10.8 0.0 copy-done
  10.8 0.0 copy-done.1
  10.8 0.2 %fusion = f32[24,384]{1,0:T(8,128)S(1)} fusion(f32[192,384]{1,0:T(8,128)S(1)} %bitcast.10, s32[192]{0:T(256)S(1)} %iota_add_fusion, s32[24]{0:T(128)S(1)} %bitcast.16), kind=kOutput, calls=%fused_computation | convolution fusion | flops 21238272 | bytes 332640 | tf_op jit(solution)/shard_map/dot_general | solution.py:329
  11.0 0.3 %collective-permute-start = (f32[24,384]{1,0:T(8,128)S(1)}, f32[24,384]{1,0:T(8,128)S(1)}, u32[]{:S(2)}, u32[]{:S(2)}) collective-permute-start(f32[24,384]{1,0:T(8,128)S(1)} %fusion), channel_id=1, source_target_pairs={{0,1},{1,0},{2,3},{3,2},{4,5},{5,4},{6,7},{7,6},{8,9},{9,8},{10,11... | collective-permute-start | bytes 110600 | tf_op jit(solution)/shard_map/ppermute | solution.py:332
  11.3 1.0 %collective-permute-done = f32[24,384]{1,0:T(8,128)S(1)} collective-permute-done((f32[24,384]{1,0:T(8,128)S(1)}, f32[24,384]{1,0:T(8,128)S(1)}, u32[]{:S(2)}, u32[]{:S(2)}) %collective-permute-start) | collective-permute-done | bytes 36896 | tf_op jit(solution)/shard_map/ppermute | solution.py:332
  12.3 1.5 %shard_map.74 = (f32[16,384]{1,0:T(8,128)S(1)}, f32[16,24]{1,0:T(8,128)S(1)}, bf16[5,208,768]{2,1,0:T(8,128)(2,1)S(1)}) custom-call(f32[24,128]{1,0:T(8,128)S(1)} %get-tuple-element.15.inv_ref, f32[24,384]{1,0:T(8,128)S(1)} %add.12.picked_ref, s32[1,1]{1,0:T(1,128)} %bitcast.9.counts_ref, s32[2]{0:T(128)} %sizes_ref.3, bf16[6,2,3840]{2,1,0:T(2,128)(2,1)} %bitcast.13, ...), custom_call_target="tpu_custom_call" | custom-call | tf_op jit(solution)/shard_map/pallas_call | solution.py:334
  13.9 5.8 %all-to-all-done = f32[32,12,1,128]{3,2,1,0:T(1,128)S(1)} async-done(((f32[32,12,1,128]{3,2,1,0:T(1,128)}), f32[32,12,1,128]{3,2,1,0:T(1,128)S(1)}, u32[]{:S(2)}, u32[]{:S(2)}) %all-to-all-start) | async-done | bytes 196640 | tf_op jit(solution)/shard_map/all_to_all | solution.py:325
  19.7 2.1 %shard_map.75 = bf16[96,2,3840]{2,1,0:T(2,128)(2,1)} custom-call(f32[384,128]{1,0:T(8,128)S(1)} %bitcast.11, f32[16,384]{1,0:T(8,128)S(1)} %get-tuple-element.18.coarse_ref, f32[16,24]{1,0:T(8,128)S(1)} %get-tuple-element.19.turned_ref, bf16[5,208,768]{2,1,0:T(8,128)(2,1)S(1)} %get-tuple-element.20.x_ref), custom_call_target="tpu_custom_call" | custom-call | tf_op jit(solution)/shard_map/pallas_call | solution.py:361
  (2 shorter events, 0.0 us)
Async XLA Ops:
  0.0 10.8 %copy-start = (f32[384,192]{0,1:T(8,128)S(1)}, f32[384,192]{0,1:T(8,128)}, u32[]{:S(2)}) copy-start(f32[384,192]{0,1:T(8,128)} %param.13) | copy-start | bytes 884740
  0.0 10.8 %copy-start.1 = (s32[1,24]{1,0:T(1,128)S(1)}, s32[1,24]{1,0:T(1,128)}, u32[]{:S(2)}) copy-start(s32[1,24]{1,0:T(1,128)} %map_ref.1) | copy-start | bytes 292
  3.4 16.3 %all-to-all-start = ((f32[32,12,1,128]{3,2,1,0:T(1,128)}), f32[32,12,1,128]{3,2,1,0:T(1,128)S(1)}, u32[]{:S(2)}, u32[]{:S(2)}) async-start(f32[32,12,1,128]{3,2,1,0:T(1,128)} %bitcast.14), calls=%async_computation | async-start | bytes 393216 | tf_op jit(solution)/shard_map/all_to_all | solution.py:325
  11.0 1.3 %collective-permute-start = (f32[24,384]{1,0:T(8,128)S(1)}, f32[24,384]{1,0:T(8,128)S(1)}, u32[]{:S(2)}, u32[]{:S(2)}) collective-permute-start(f32[24,384]{1,0:T(8,128)S(1)} %fusion), channel_id=1, source_target_pairs={{0,1},{1,0},{2,3},{3,2},{4,5},{5,4},{6,7},{7,6},{8,9},{9,8},{10,11... | collective-permute-start | bytes 110600 | tf_op jit(solution)/shard_map/ppermute | solution.py:332

commit v8 on v7

--- a/solution.py
+++ b/solution.py
@@ -98,13 +98,14 @@
 
 
 def first_kernel(rhs, counts_ref, sizes_ref, kernel_ref, lower_ref, map_ref, duals_ref,
-                 send_ref, inv_ref,
-                 count_s, size_s, raw_ref, tri_ref, row_ref, x_ref, acc_ref, mix_ref, block_ref, sol_ref, sems, small_sems):
+                 send_ref, inv_ref, x_ref,
+                 count_s, size_s, raw_ref, tri_ref, row_ref, acc_ref, mix_ref, block_ref, sol_ref, sems, small_sems):
     modes, sub, width = kernel_ref.shape
     rows = modes * sub
     ck = lower_ref.shape[0]
     lanes = inv_ref.shape[1]
-    count, _, step = x_ref.shape
+    count, deep, step = x_ref.shape
+    flat = rhs * sub
     copy = slab_copies(duals_ref, x_ref, sems)
     small = [
         pltpu.make_async_copy(src, dst, small_sems.at[n])
@@ -145,6 +146,9 @@
     for one in small[2:]:
         one.wait()
     masked = mask_kernel(raw_ref, count_s, size_s, sub)
+    for n in range(count):
+        x_ref[n, flat:, :] = jnp.zeros((deep - flat, step), BF16)
+        x_ref[n, flat : flat + rows, :] = masked[:, n * step : (n + 1) * step]
     acc_ref[...] = jnp.zeros_like(acc_ref)
     cut = up(rhs * sub // 2, 16)
     halves = [(0, cut), (cut, rhs * sub)]
@@ -169,39 +173,16 @@
         send_ref[pl.ds(d * rows * group, rows * group), :] = block
 
 
-def middle_kernel(rhs, inv_ref, picked_ref, counts_ref, sizes_ref, kernel_ref, duals_ref,
-                  coarse_ref, turned_ref, x_ref,
-                  count_s, size_s, raw_ref, turn_ref, sems, small_sems):
-    modes, sub, width = kernel_ref.shape
-    rows = modes * sub
+def middle_kernel(rhs, sub, inv_ref, picked_ref, coarse_ref, turned_ref, turn_ref):
     ck = picked_ref.shape[0]
-    count, deep, step = x_ref.shape
-    flat = duals_ref.shape[0] * sub
-    copy = slab_copies(duals_ref, x_ref, sems)
-    small = [
-        pltpu.make_async_copy(src, dst, small_sems.at[n])
-        for n, (src, dst) in enumerate(
-            ((counts_ref, count_s), (sizes_ref, size_s), (kernel_ref.reshape(rows, width), raw_ref))
-        )
-    ]
-    for one in small:
-        one.start()
-    for n in range(count):
-        copy(n).start()
+    rows = ck // lax.axis_size("clus")
+    modes = rows // sub
     place = lax.axis_index("clus").astype(jnp.int32)
     turn_ref[...] = inv_ref[:, rhs : rhs + ck].T
     turned_ref[...] = jnp.zeros_like(turned_ref)
     for s in range(sub):
         turned_ref[pl.ds(s, modes, stride=sub), :] = turn_ref[pl.ds(place * rows + s * modes, modes), :]
     coarse_ref[...] = lax.dot_general(turned_ref[...], picked_ref[...], NN, precision=HI, preferred_element_type=F32)
-    for one in small:
-        one.wait()
-    masked = mask_kernel(raw_ref, count_s, size_s, sub)
-    for n in range(count):
-        x_ref[n, flat:, :] = jnp.zeros((deep - flat, step), BF16)
-        x_ref[n, flat : flat + rows, :] = masked[:, n * step : (n + 1) * step]
-    for n in range(count):
-        copy(n).wait()
 
 
 def write_out(corr, sub, x_ref, out_ref, corr_ref, o_ref, sems):
@@ -299,18 +280,17 @@
     small_enough = total * max(total, gk) <= 2**20
     OUT = pltpu.VMEM if small_enough else jax.ShapeDtypeStruct
 
-    send, inv = pl.pallas_call(
+    send, inv, x = pl.pallas_call(
         functools.partial(first_kernel, rhs),
-        out_shape=(jax.ShapeDtypeStruct((total, lanes), F32), OUT((ck, lanes), F32)),
+        out_shape=(jax.ShapeDtypeStruct((total, lanes), F32), OUT((ck, lanes), F32), OUT(deeper, BF16)),
         in_specs=[HBM] * 6,
-        out_specs=(VMEM, VMEM),
+        out_specs=(VMEM, VMEM, VMEM),
         scratch_shapes=[
             pltpu.SMEM((1, 1), jnp.int32),
             pltpu.SMEM((sub,), jnp.int32),
             pltpu.VMEM((rows, width), BF16),
             pltpu.VMEM((ck, ck), F32),
             pltpu.VMEM((1, ck), jnp.int32),
-            pltpu.VMEM(slabs, BF16),
             pltpu.VMEM((padded, rhs * sub), F32),
             pltpu.VMEM((lanes // LANES, padded, LANES), F32),
             pltpu.VMEM((rows, lanes), F32),
@@ -331,25 +311,14 @@
     for shift in range(1, members):
         picked = picked + lax.ppermute(part, "clus", [(i, (i + shift) % members) for i in range(members)])
     params = pltpu.CompilerParams(vmem_limit_bytes=LAST_LIMIT)
-    coarse, turned, x = pl.pallas_call(
-        functools.partial(middle_kernel, rhs),
-        out_shape=(
-            OUT((padded, gk), F32),
-            OUT((padded, ck), F32),
-            OUT(deeper, BF16),
-        ),
-        in_specs=[VMEM, VMEM] + [HBM] * 4,
-        out_specs=(VMEM,) * 3,
-        scratch_shapes=[
-            pltpu.SMEM((1, 1), jnp.int32),
-            pltpu.SMEM((sub,), jnp.int32),
-            pltpu.VMEM((rows, width), BF16),
-            pltpu.VMEM((ck, ck), F32),
-            pltpu.SemaphoreType.DMA((count,)),
-            pltpu.SemaphoreType.DMA((3,)),
-        ],
+    coarse, turned = pl.pallas_call(
+        functools.partial(middle_kernel, rhs, sub),
+        out_shape=(OUT((padded, gk), F32), OUT((padded, ck), F32)),
+        in_specs=[VMEM, VMEM],
+        out_specs=(VMEM, VMEM),
+        scratch_shapes=[pltpu.VMEM((ck, ck), F32)],
         compiler_params=params,
-    )(inv, picked, counts, sizes, modes_first, vectors)
+    )(inv, picked)
 
     out_shape = jax.ShapeDtypeStruct(duals.shape, BF16)
     scratch = [

time: 22.1 us -> 22.1 us (level)
  waiting for transfers between devices: 6.8 us -> 8.09 us
  Pallas kernels: 6.34 us -> 5.06 us
    all_to_all x1, waiting for transfers between devices: 5.84 us -> 7.13 us  [per_device(): recv = lax.all_to_all(spread, ('wide', 'clus'), 0, 0)]
    pallas_call x1, Pallas kernels: 1.55 us -> 0.27 us  [per_device(): pl.pallas_call(functools.partial(middle_kernel, rhs, sub), out_shape=(OUT...]
  transfers between devices with their start and end apart: 2 -> 2, of which waited for: 2 -> 2; matrix products, arithmetic and copies ran while one was open for 1% -> 1% of each run, Pallas kernels for 7% -> 1%
where the time goes in v8:
time: 22.1 us; the launch traced here: 21.8 us
  waiting for transfers between devices  8.09 us (37%)
  starting transfers between devices  7.64 us (35%)
  Pallas kernels  5.06 us (23%)
  between operations  0.74 us (3%)
  matrix products  0.23 us (1%)
    all_to_all x1, starting transfers between devices, per_device(): recv = lax.all_to_all(spread, ('wide', 'clus'), 0, 0)  7.33 us
    all_to_all x1, waiting for transfers between devices, per_device(): recv = lax.all_to_all(spread, ('wide', 'clus'), 0, 0)  7.13 us
    pallas_call x1, Pallas kernels, per_device(): pl.pallas_call(functools.partial(first_kernel, rhs), out_shape=(jax.Shape...  2.71 us
    pallas_call x1, Pallas kernels, per_device(): pl.pallas_call(functools.partial(last_kernel, rhs, sub), out_shape=out_sh...  2.08 us
    ppermute x1, waiting for transfers between devices, per_device(): lax.ppermute(part, 'clus', [(i, (i + shift) % members) for i in range(mem...  0.96 us
  transfers between devices with their start and end apart: 2, of which 2 were waited for; matrix products, arithmetic and copies ran while one was open for 1% of the time, Pallas kernels for 1%

profile of v8, /device:TPU:0, one launch (start us, length us, event | category | flops | bytes accessed | tf_op | source)
XLA Modules:
  0.0 21.8 jit_solution(14997696096801205879)
XLA Ops:
  0.0 0.0 copy-start
  0.0 0.0 copy-start.1
  0.7 2.7 %shard_map.73 = (f32[384,128]{1,0:T(8,128)}, f32[24,128]{1,0:T(8,128)S(1)}, bf16[5,208,768]{2,1,0:T(8,128)(2,1)S(1)}) custom-call(s32[1,1]{1,0:T(1,128)} %bitcast.8.counts_ref, s32[2]{0:T(128)} %sizes_ref.1, bf16[6,2,3840]{2,1,0:T(2,128)(2,1)} %bitcast.12, f32[24,24]{1,0:T(8,128)} %bitcast.13, s32[1,24]{1,0:T(1,128)} %map_ref.1, bf16[96,2,3840]{2,1,0:T(2,128)(2,1)} %duals_ref.1), custom_call_target="tpu_custom_call" | custom-call | tf_op jit(solution)/shard_map/pallas_call | solution.py:283
  3.4 7.3 %all-to-all-start = ((f32[32,12,1,128]{3,2,1,0:T(1,128)}), f32[32,12,1,128]{3,2,1,0:T(1,128)S(1)}, u32[]{:S(2)}, u32[]{:S(2)}) async-start(f32[32,12,1,128]{3,2,1,0:T(1,128)} %bitcast.11), calls=%async_computation | async-start | bytes 393216 | tf_op jit(solution)/shard_map/all_to_all | solution.py:305
  10.8 0.0 copy-done
  10.8 0.0 copy-done.1
  10.8 0.2 %fusion = f32[24,384]{1,0:T(8,128)S(1)} fusion(f32[192,384]{1,0:T(8,128)S(1)} %bitcast.9, s32[192]{0:T(256)S(1)} %iota_add_fusion, s32[24]{0:T(128)S(1)} %bitcast.14), kind=kOutput, calls=%fused_computation | convolution fusion | flops 21238272 | bytes 332640 | tf_op jit(solution)/shard_map/dot_general | solution.py:309
  11.0 0.3 %collective-permute-start = (f32[24,384]{1,0:T(8,128)S(1)}, f32[24,384]{1,0:T(8,128)S(1)}, u32[]{:S(2)}, u32[]{:S(2)}) collective-permute-start(f32[24,384]{1,0:T(8,128)S(1)} %fusion), channel_id=1, source_target_pairs={{0,1},{1,0},{2,3},{3,2},{4,5},{5,4},{6,7},{7,6},{8,9},{9,8},{10,11... | collective-permute-start | bytes 110600 | tf_op jit(solution)/shard_map/ppermute | solution.py:312
  11.3 1.0 %collective-permute-done = f32[24,384]{1,0:T(8,128)S(1)} collective-permute-done((f32[24,384]{1,0:T(8,128)S(1)}, f32[24,384]{1,0:T(8,128)S(1)}, u32[]{:S(2)}, u32[]{:S(2)}) %collective-permute-start) | collective-permute-done | bytes 36896 | tf_op jit(solution)/shard_map/ppermute | solution.py:312
  12.3 0.3 %shard_map.74 = (f32[16,384]{1,0:T(8,128)S(1)}, f32[16,24]{1,0:T(8,128)S(1)}) custom-call(f32[24,128]{1,0:T(8,128)S(1)} %get-tuple-element.15.inv_ref, f32[24,384]{1,0:T(8,128)S(1)} %add.12.picked_ref), custom_call_target="tpu_custom_call" | custom-call | tf_op jit(solution)/shard_map/pallas_call | solution.py:314
  12.6 7.1 %all-to-all-done = f32[32,12,1,128]{3,2,1,0:T(1,128)S(1)} async-done(((f32[32,12,1,128]{3,2,1,0:T(1,128)}), f32[32,12,1,128]{3,2,1,0:T(1,128)S(1)}, u32[]{:S(2)}, u32[]{:S(2)}) %all-to-all-start) | async-done | bytes 196640 | tf_op jit(solution)/shard_map/all_to_all | solution.py:305
  19.7 2.1 %shard_map.75 = bf16[96,2,3840]{2,1,0:T(2,128)(2,1)} custom-call(f32[384,128]{1,0:T(8,128)S(1)} %bitcast.10, f32[16,384]{1,0:T(8,128)S(1)} %get-tuple-element.18.coarse_ref, f32[16,24]{1,0:T(8,128)S(1)} %get-tuple-element.19.turned_ref, bf16[5,208,768]{2,1,0:T(8,128)(2,1)S(1)} %get-tuple-element.20.x_ref), custom_call_target="tpu_custom_call" | custom-call | tf_op jit(solution)/shard_map/pallas_call | solution.py:330
  (2 shorter events, 0.0 us)
Async XLA Ops:
  0.0 10.8 %copy-start = (f32[384,192]{0,1:T(8,128)S(1)}, f32[384,192]{0,1:T(8,128)}, u32[]{:S(2)}) copy-start(f32[384,192]{0,1:T(8,128)} %param.13) | copy-start | bytes 884740
  0.0 10.8 %copy-start.1 = (s32[1,24]{1,0:T(1,128)S(1)}, s32[1,24]{1,0:T(1,128)}, u32[]{:S(2)}) copy-start(s32[1,24]{1,0:T(1,128)} %map_ref.1) | copy-start | bytes 292
  3.4 16.3 %all-to-all-start = ((f32[32,12,1,128]{3,2,1,0:T(1,128)}), f32[32,12,1,128]{3,2,1,0:T(1,128)S(1)}, u32[]{:S(2)}, u32[]{:S(2)}) async-start(f32[32,12,1,128]{3,2,1,0:T(1,128)} %bitcast.11), calls=%async_computation | async-start | bytes 393216 | tf_op jit(solution)/shard_map/all_to_all | solution.py:305
  11.0 1.3 %collective-permute-start = (f32[24,384]{1,0:T(8,128)S(1)}, f32[24,384]{1,0:T(8,128)S(1)}, u32[]{:S(2)}, u32[]{:S(2)}) collective-permute-start(f32[24,384]{1,0:T(8,128)S(1)} %fusion), channel_id=1, source_target_pairs={{0,1},{1,0},{2,3},{3,2},{4,5},{5,4},{6,7},{7,6},{8,9},{9,8},{10,11... | collective-permute-start | bytes 110600 | tf_op jit(solution)/shard_map/ppermute | solution.py:312

commit v9 on v8

--- a/solution.py
+++ b/solution.py
@@ -17,7 +17,7 @@
 HBM = pl.BlockSpec(memory_space=pltpu.HBM)
 FIRST_LIMIT = 60 * 2**20
 LAST_LIMIT = 20 * 2**20
-AHEAD = 8
+AHEAD = 6
 
 
 def iota(shape, dim):
@@ -99,7 +99,7 @@
 
 def first_kernel(rhs, counts_ref, sizes_ref, kernel_ref, lower_ref, map_ref, duals_ref,
                  send_ref, inv_ref, x_ref,
-                 count_s, size_s, raw_ref, tri_ref, row_ref, acc_ref, mix_ref, block_ref, sol_ref, sems, small_sems):
+                 count_s, size_s, raw_ref, tri_ref, row_ref, acc_ref, block_ref, sol_ref, sems, small_sems):
     modes, sub, width = kernel_ref.shape
     rows = modes * sub
     ck = lower_ref.shape[0]
@@ -131,7 +131,9 @@
     eye = iota((ck, ck), 0) == iota((ck, ck), 1)
     scale = 1.0 / jnp.sum(jnp.where(eye, lower, 0.0), axis=1, keepdims=True)
     below = jnp.where(iota((ck, ck), 0) > iota((ck, ck), 1), lower * scale, 0.0)
-    sol = jnp.where(iota((ck, lanes), 1) == rhs + iota((ck, lanes), 0), scale, 0.0)
+    order = iota((ck, lanes), 0)
+    order = order // rows * rows + order % modes * sub + order % rows // modes
+    sol = jnp.where(iota((ck, lanes), 1) == rhs + order, scale, 0.0)
     for i in range(ck - 1):
         sol = sol - below[:, i : i + 1] * sol[i : i + 1, :]
     inv_ref[...] = sol
@@ -161,28 +163,28 @@
     same = iota((rows, rhs * sub), 0) % sub == iota((rows, rhs * sub), 1) % sub
     acc_ref[:rows, :] = jnp.where(same, total, 0.0)
     mixed = dot_exact(acc_ref[...], rows_of_slots(sub, rhs, lanes), NN)
-    for c in range(lanes // LANES):
-        cols = slice(c * LANES, (c + 1) * LANES)
-        mix_ref[c] = mixed[:, cols]
-        for s in range(sub):
-            here = slice(s * modes, (s + 1) * modes)
-            block_ref[here, cols] += mix_ref[c, pl.ds(s, modes, stride=sub), :]
+    block = block_ref[...] + mixed[:rows, :]
     group = 2 if send_ref.shape[0] % (2 * rows) == 0 else 1
-    block = jnp.concatenate([block_ref[...]] * group, axis=0)
+    block = jnp.concatenate([block] * group, axis=0)
     for d in range(send_ref.shape[0] // (rows * group)):
         send_ref[pl.ds(d * rows * group, rows * group), :] = block
 
 
-def middle_kernel(rhs, sub, inv_ref, picked_ref, coarse_ref, turned_ref, turn_ref):
+def middle_kernel(rhs, rows, inv_ref, picked_ref, coarse_ref, turned_ref, turn_ref, own_ref=None):
     ck = picked_ref.shape[0]
-    rows = ck // lax.axis_size("clus")
-    modes = rows // sub
     place = lax.axis_index("clus").astype(jnp.int32)
     turn_ref[...] = inv_ref[:, rhs : rhs + ck].T
     turned_ref[...] = jnp.zeros_like(turned_ref)
-    for s in range(sub):
-        turned_ref[pl.ds(s, modes, stride=sub), :] = turn_ref[pl.ds(place * rows + s * modes, modes), :]
+    turned_ref[:rows, :] = turn_ref[pl.ds(place * rows, rows), :]
     coarse_ref[...] = lax.dot_general(turned_ref[...], picked_ref[...], NN, precision=HI, preferred_element_type=F32)
+    if own_ref is not None:
+        cluster = lax.axis_index("wide").astype(jnp.int32)
+        for w in range(own_ref.shape[1] // ck):
+            own_ref[:, w * ck : (w + 1) * ck] = jnp.where(w == cluster, turned_ref[...], 0.0)
+
+
+def middle_kernel_small(rhs, rows, inv_ref, picked_ref, coarse_ref, own_ref, turn_ref, turned_ref):
+    middle_kernel(rhs, rows, inv_ref, picked_ref, coarse_ref, turned_ref, turn_ref, own_ref)
 
 
 def write_out(corr, sub, x_ref, out_ref, corr_ref, o_ref, sems):
@@ -233,11 +235,9 @@
     return spans
 
 
-def last_kernel(rhs, sub, recv_ref, coarse_ref, turned_ref, x_ref, out_ref, block_ref, sum_ref, corr_ref, o_ref, sems):
+def last_kernel(rhs, sub, ck, recv_ref, coarse_ref, own_ref, x_ref, out_ref, block_ref, sum_ref, corr_ref, o_ref, sems):
     total = recv_ref.shape[0]
     gk = coarse_ref.shape[1]
-    ck = turned_ref.shape[1]
-    cluster = lax.axis_index("wide").astype(jnp.int32)
     done = 0
     for low, high, part in block_product(recv_ref, rhs, ck, block_ref):
         if low < done:
@@ -247,8 +247,7 @@
     target = recv_ref[:, rhs + ck : rhs + ck + 1].astype(jnp.int32)
     hot = (target == iota((total, gk), 1)).astype(F32).astype(BF16)
     taken = dot_exact(coarse_ref[...], hot, NT)
-    mine = sum_ref[pl.ds(pl.multiple_of(cluster * ck, ck), ck), :]
-    corr = dot_parts(turned_ref[...], mine, NN) - dot_parts(taken, sum_ref[...], NN)
+    corr = dot_parts(own_ref[...] - taken, sum_ref[...], NN)
     write_out(corr.astype(BF16), sub, x_ref, out_ref, corr_ref, o_ref, sems)
 
 
@@ -292,7 +291,6 @@
             pltpu.VMEM((ck, ck), F32),
             pltpu.VMEM((1, ck), jnp.int32),
             pltpu.VMEM((padded, rhs * sub), F32),
-            pltpu.VMEM((lanes // LANES, padded, LANES), F32),
             pltpu.VMEM((rows, lanes), F32),
             pltpu.VMEM((lanes // LANES, ck, LANES), F32),
             pltpu.SemaphoreType.DMA((count,)),
@@ -312,11 +310,11 @@
         picked = picked + lax.ppermute(part, "clus", [(i, (i + shift) % members) for i in range(members)])
     params = pltpu.CompilerParams(vmem_limit_bytes=LAST_LIMIT)
     coarse, turned = pl.pallas_call(
-        functools.partial(middle_kernel, rhs, sub),
-        out_shape=(OUT((padded, gk), F32), OUT((padded, ck), F32)),
+        functools.partial(middle_kernel_small if small_enough else middle_kernel, rhs, rows),
+        out_shape=(OUT((padded, gk), F32), OUT((padded, total if small_enough else ck), F32)),
         in_specs=[VMEM, VMEM],
         out_specs=(VMEM, VMEM),
-        scratch_shapes=[pltpu.VMEM((ck, ck), F32)],
+        scratch_shapes=[pltpu.VMEM((ck, ck), F32), pltpu.VMEM((padded, ck), F32)][: 1 + small_enough],
         compiler_params=params,
     )(inv, picked)
 
@@ -328,7 +326,7 @@
     ]
     if small_enough:
         return pl.pallas_call(
-            functools.partial(last_kernel, rhs, sub),
+            functools.partial(last_kernel, rhs, sub, ck),
             out_shape=out_shape,
             in_specs=[VMEM] * 4,
             out_specs=HBM,

time: 22.1 us -> 22.1 us (level)
  no operation moved by 1% of the time
where the time goes in v9:
time: 22.1 us; the launch traced here: 21.8 us
  waiting for transfers between devices  8.05 us (36%)
  starting transfers between devices  7.64 us (35%)
  Pallas kernels  5.14 us (23%)
  between operations  0.74 us (3%)
  matrix products  0.23 us (1%)
    all_to_all x1, starting transfers between devices, per_device(): recv = lax.all_to_all(spread, ('wide', 'clus'), 0, 0)  7.33 us
    all_to_all x1, waiting for transfers between devices, per_device(): recv = lax.all_to_all(spread, ('wide', 'clus'), 0, 0)  7.09 us
    pallas_call x1, Pallas kernels, per_device(): pl.pallas_call(functools.partial(first_kernel, rhs), out_shape=(jax.Shape...  2.7 us
    pallas_call x1, Pallas kernels, per_device(): pl.pallas_call(functools.partial(last_kernel, rhs, sub, ck), out_shape=ou...  2.14 us
    ppermute x1, waiting for transfers between devices, per_device(): lax.ppermute(part, 'clus', [(i, (i + shift) % members) for i in range(mem...  0.96 us
  transfers between devices with their start and end apart: 2, of which 2 were waited for; matrix products, arithmetic and copies ran while one was open for 1% of the time, Pallas kernels for 1%

profile of v9, /device:TPU:0, one launch (start us, length us, event | category | flops | bytes accessed | tf_op | source)
XLA Modules:
  0.0 21.8 jit_solution(4967937337967579538)
XLA Ops:
  0.0 0.0 copy-start
  0.0 0.0 copy-start.1
  0.7 2.7 %shard_map.73 = (f32[384,128]{1,0:T(8,128)}, f32[24,128]{1,0:T(8,128)S(1)}, bf16[5,208,768]{2,1,0:T(8,128)(2,1)S(1)}) custom-call(s32[1,1]{1,0:T(1,128)} %bitcast.8.counts_ref, s32[2]{0:T(128)} %sizes_ref.1, bf16[6,2,3840]{2,1,0:T(2,128)(2,1)} %bitcast.12, f32[24,24]{1,0:T(8,128)} %bitcast.13, s32[1,24]{1,0:T(1,128)} %map_ref.1, bf16[96,2,3840]{2,1,0:T(2,128)(2,1)} %duals_ref.1), custom_call_target="tpu_custom_call" | custom-call | tf_op jit(solution)/shard_map/pallas_call | solution.py:282
  3.4 7.3 %all-to-all-start = ((f32[32,12,1,128]{3,2,1,0:T(1,128)}), f32[32,12,1,128]{3,2,1,0:T(1,128)S(1)}, u32[]{:S(2)}, u32[]{:S(2)}) async-start(f32[32,12,1,128]{3,2,1,0:T(1,128)} %bitcast.11), calls=%async_computation | async-start | bytes 393216 | tf_op jit(solution)/shard_map/all_to_all | solution.py:303
  10.8 0.0 copy-done
  10.8 0.0 copy-done.1
  10.8 0.2 %fusion = f32[24,384]{1,0:T(8,128)S(1)} fusion(f32[192,384]{1,0:T(8,128)S(1)} %bitcast.9, s32[192]{0:T(256)S(1)} %iota_add_fusion, s32[24]{0:T(128)S(1)} %bitcast.14), kind=kOutput, calls=%fused_computation | convolution fusion | flops 21238272 | bytes 332640 | tf_op jit(solution)/shard_map/dot_general | solution.py:307
  11.0 0.3 %collective-permute-start = (f32[24,384]{1,0:T(8,128)S(1)}, f32[24,384]{1,0:T(8,128)S(1)}, u32[]{:S(2)}, u32[]{:S(2)}) collective-permute-start(f32[24,384]{1,0:T(8,128)S(1)} %fusion), channel_id=1, source_target_pairs={{0,1},{1,0},{2,3},{3,2},{4,5},{5,4},{6,7},{7,6},{8,9},{9,8},{10,11... | collective-permute-start | bytes 110600 | tf_op jit(solution)/shard_map/ppermute | solution.py:310
  11.3 1.0 %collective-permute-done = f32[24,384]{1,0:T(8,128)S(1)} collective-permute-done((f32[24,384]{1,0:T(8,128)S(1)}, f32[24,384]{1,0:T(8,128)S(1)}, u32[]{:S(2)}, u32[]{:S(2)}) %collective-permute-start) | collective-permute-done | bytes 36896 | tf_op jit(solution)/shard_map/ppermute | solution.py:310
  12.3 0.3 %shard_map.74 = (f32[16,384]{1,0:T(8,128)S(1)}, f32[16,384]{1,0:T(8,128)S(1)}) custom-call(f32[24,128]{1,0:T(8,128)S(1)} %get-tuple-element.15.inv_ref, f32[24,384]{1,0:T(8,128)S(1)} %add.12.picked_ref), custom_call_target="tpu_custom_call" | custom-call | tf_op jit(solution)/shard_map/pallas_call | solution.py:312
  12.6 7.1 %all-to-all-done = f32[32,12,1,128]{3,2,1,0:T(1,128)S(1)} async-done(((f32[32,12,1,128]{3,2,1,0:T(1,128)}), f32[32,12,1,128]{3,2,1,0:T(1,128)S(1)}, u32[]{:S(2)}, u32[]{:S(2)}) %all-to-all-start) | async-done | bytes 196640 | tf_op jit(solution)/shard_map/all_to_all | solution.py:303
  19.7 2.1 %shard_map.75 = bf16[96,2,3840]{2,1,0:T(2,128)(2,1)} custom-call(f32[384,128]{1,0:T(8,128)S(1)} %bitcast.10, f32[16,384]{1,0:T(8,128)S(1)} %get-tuple-element.18.coarse_ref, f32[16,384]{1,0:T(8,128)S(1)} %get-tuple-element.19.own_ref, bf16[5,208,768]{2,1,0:T(8,128)(2,1)S(1)} %get-tuple-element.20.x_ref), custom_call_target="tpu_custom_call" | custom-call | tf_op jit(solution)/shard_map/pallas_call | solution.py:328
  (2 shorter events, 0.0 us)
Async XLA Ops:
  0.0 10.8 %copy-start = (f32[384,192]{0,1:T(8,128)S(1)}, f32[384,192]{0,1:T(8,128)}, u32[]{:S(2)}) copy-start(f32[384,192]{0,1:T(8,128)} %param.13) | copy-start | bytes 884740
  0.0 10.8 %copy-start.1 = (s32[1,24]{1,0:T(1,128)S(1)}, s32[1,24]{1,0:T(1,128)}, u32[]{:S(2)}) copy-start(s32[1,24]{1,0:T(1,128)} %map_ref.1) | copy-start | bytes 292
  3.4 16.3 %all-to-all-start = ((f32[32,12,1,128]{3,2,1,0:T(1,128)}), f32[32,12,1,128]{3,2,1,0:T(1,128)S(1)}, u32[]{:S(2)}, u32[]{:S(2)}) async-start(f32[32,12,1,128]{3,2,1,0:T(1,128)} %bitcast.11), calls=%async_computation | async-start | bytes 393216 | tf_op jit(solution)/shard_map/all_to_all | solution.py:303
  11.0 1.3 %collective-permute-start = (f32[24,384]{1,0:T(8,128)S(1)}, f32[24,384]{1,0:T(8,128)S(1)}, u32[]{:S(2)}, u32[]{:S(2)}) collective-permute-start(f32[24,384]{1,0:T(8,128)S(1)} %fusion), channel_id=1, source_target_pairs={{0,1},{1,0},{2,3},{3,2},{4,5},{5,4},{6,7},{7,6},{8,9},{9,8},{10,11... | collective-permute-start | bytes 110600 | tf_op jit(solution)/shard_map/ppermute | solution.py:310

commit v10 on v9

--- a/solution.py
+++ b/solution.py
@@ -222,15 +222,17 @@
 
 def block_product(recv_ref, rhs, ck, block_ref):
     total = recv_ref.shape[0]
-    block_ref[...] = jnp.zeros_like(block_ref)
+    bounds = []
+    for start in range(0, total, LANES):
+        stop = min(start + LANES, total)
+        bounds.append((start, stop, start // ck * ck // 16 * 16, min(up(up(stop, ck), 16), total)))
+    for start, stop, low, high in bounds:
+        block_ref[low:high, start:stop] = jnp.zeros((high - low, stop - start), F32)
     for w in range(total // ck):
         here = slice(w * ck, (w + 1) * ck)
         block_ref[here, here] = recv_ref[here, rhs : rhs + ck]
     spans = []
-    for start in range(0, total, LANES):
-        stop = min(start + LANES, total)
-        low = start // ck * ck // 16 * 16
-        high = min(up(up(stop, ck), 16), total)
+    for start, stop, low, high in bounds:
         spans.append((low, high, dot_parts(block_ref[low:high, start:stop], recv_ref[start:stop, :rhs], NN)))
     return spans
 

time: 22.1 us -> 22.1 us (level)
  no operation moved by 1% of the time
where the time goes in v10:
time: 22.1 us; the launch traced here: 21.8 us
  waiting for transfers between devices  8.05 us (36%)
  starting transfers between devices  7.64 us (35%)
  Pallas kernels  5.15 us (23%)
  between operations  0.74 us (3%)
  matrix products  0.23 us (1%)
    all_to_all x1, starting transfers between devices, per_device(): recv = lax.all_to_all(spread, ('wide', 'clus'), 0, 0)  7.33 us
    all_to_all x1, waiting for transfers between devices, per_device(): recv = lax.all_to_all(spread, ('wide', 'clus'), 0, 0)  7.09 us
    pallas_call x1, Pallas kernels, per_device(): pl.pallas_call(functools.partial(first_kernel, rhs), out_shape=(jax.Shape...  2.7 us
    pallas_call x1, Pallas kernels, per_device(): pl.pallas_call(functools.partial(last_kernel, rhs, sub, ck), out_shape=ou...  2.14 us
    ppermute x1, waiting for transfers between devices, per_device(): lax.ppermute(part, 'clus', [(i, (i + shift) % members) for i in range(mem...  0.96 us
  transfers between devices with their start and end apart: 2, of which 2 were waited for; matrix products, arithmetic and copies ran while one was open for 1% of the time, Pallas kernels for 1%

profile of v10, /device:TPU:0, one launch (start us, length us, event | category | flops | bytes accessed | tf_op | source)
XLA Modules:
  0.0 21.8 jit_solution(11379001970645148658)
XLA Ops:
  0.0 0.0 copy-start
  0.0 0.0 copy-start.1
  0.7 2.7 %shard_map.73 = (f32[384,128]{1,0:T(8,128)}, f32[24,128]{1,0:T(8,128)S(1)}, bf16[5,208,768]{2,1,0:T(8,128)(2,1)S(1)}) custom-call(s32[1,1]{1,0:T(1,128)} %bitcast.8.counts_ref, s32[2]{0:T(128)} %sizes_ref.1, bf16[6,2,3840]{2,1,0:T(2,128)(2,1)} %bitcast.12, f32[24,24]{1,0:T(8,128)} %bitcast.13, s32[1,24]{1,0:T(1,128)} %map_ref.1, bf16[96,2,3840]{2,1,0:T(2,128)(2,1)} %duals_ref.1), custom_call_target="tpu_custom_call" | custom-call | tf_op jit(solution)/shard_map/pallas_call | solution.py:284
  3.4 7.3 %all-to-all-start = ((f32[32,12,1,128]{3,2,1,0:T(1,128)}), f32[32,12,1,128]{3,2,1,0:T(1,128)S(1)}, u32[]{:S(2)}, u32[]{:S(2)}) async-start(f32[32,12,1,128]{3,2,1,0:T(1,128)} %bitcast.11), calls=%async_computation | async-start | bytes 393216 | tf_op jit(solution)/shard_map/all_to_all | solution.py:305
  10.8 0.0 copy-done
  10.8 0.0 copy-done.1
  10.8 0.2 %fusion = f32[24,384]{1,0:T(8,128)S(1)} fusion(f32[192,384]{1,0:T(8,128)S(1)} %bitcast.9, s32[192]{0:T(256)S(1)} %iota_add_fusion, s32[24]{0:T(128)S(1)} %bitcast.14), kind=kOutput, calls=%fused_computation | convolution fusion | flops 21238272 | bytes 332640 | tf_op jit(solution)/shard_map/dot_general | solution.py:309
  11.0 0.3 %collective-permute-start = (f32[24,384]{1,0:T(8,128)S(1)}, f32[24,384]{1,0:T(8,128)S(1)}, u32[]{:S(2)}, u32[]{:S(2)}) collective-permute-start(f32[24,384]{1,0:T(8,128)S(1)} %fusion), channel_id=1, source_target_pairs={{0,1},{1,0},{2,3},{3,2},{4,5},{5,4},{6,7},{7,6},{8,9},{9,8},{10,11... | collective-permute-start | bytes 110600 | tf_op jit(solution)/shard_map/ppermute | solution.py:312
  11.3 1.0 %collective-permute-done = f32[24,384]{1,0:T(8,128)S(1)} collective-permute-done((f32[24,384]{1,0:T(8,128)S(1)}, f32[24,384]{1,0:T(8,128)S(1)}, u32[]{:S(2)}, u32[]{:S(2)}) %collective-permute-start) | collective-permute-done | bytes 36896 | tf_op jit(solution)/shard_map/ppermute | solution.py:312
  12.3 0.3 %shard_map.74 = (f32[16,384]{1,0:T(8,128)S(1)}, f32[16,384]{1,0:T(8,128)S(1)}) custom-call(f32[24,128]{1,0:T(8,128)S(1)} %get-tuple-element.15.inv_ref, f32[24,384]{1,0:T(8,128)S(1)} %add.12.picked_ref), custom_call_target="tpu_custom_call" | custom-call | tf_op jit(solution)/shard_map/pallas_call | solution.py:314
  12.6 7.1 %all-to-all-done = f32[32,12,1,128]{3,2,1,0:T(1,128)S(1)} async-done(((f32[32,12,1,128]{3,2,1,0:T(1,128)}), f32[32,12,1,128]{3,2,1,0:T(1,128)S(1)}, u32[]{:S(2)}, u32[]{:S(2)}) %all-to-all-start) | async-done | bytes 196640 | tf_op jit(solution)/shard_map/all_to_all | solution.py:305
  19.7 2.1 %shard_map.75 = bf16[96,2,3840]{2,1,0:T(2,128)(2,1)} custom-call(f32[384,128]{1,0:T(8,128)S(1)} %bitcast.10, f32[16,384]{1,0:T(8,128)S(1)} %get-tuple-element.18.coarse_ref, f32[16,384]{1,0:T(8,128)S(1)} %get-tuple-element.19.own_ref, bf16[5,208,768]{2,1,0:T(8,128)(2,1)S(1)} %get-tuple-element.20.x_ref), custom_call_target="tpu_custom_call" | custom-call | tf_op jit(solution)/shard_map/pallas_call | solution.py:330
  (2 shorter events, 0.0 us)
Async XLA Ops:
  0.0 10.8 %copy-start = (f32[384,192]{0,1:T(8,128)S(1)}, f32[384,192]{0,1:T(8,128)}, u32[]{:S(2)}) copy-start(f32[384,192]{0,1:T(8,128)} %param.13) | copy-start | bytes 884740
  0.0 10.8 %copy-start.1 = (s32[1,24]{1,0:T(1,128)S(1)}, s32[1,24]{1,0:T(1,128)}, u32[]{:S(2)}) copy-start(s32[1,24]{1,0:T(1,128)} %map_ref.1) | copy-start | bytes 292
  3.4 16.3 %all-to-all-start = ((f32[32,12,1,128]{3,2,1,0:T(1,128)}), f32[32,12,1,128]{3,2,1,0:T(1,128)S(1)}, u32[]{:S(2)}, u32[]{:S(2)}) async-start(f32[32,12,1,128]{3,2,1,0:T(1,128)} %bitcast.11), calls=%async_computation | async-start | bytes 393216 | tf_op jit(solution)/shard_map/all_to_all | solution.py:305
  11.0 1.3 %collective-permute-start = (f32[24,384]{1,0:T(8,128)S(1)}, f32[24,384]{1,0:T(8,128)S(1)}, u32[]{:S(2)}, u32[]{:S(2)}) collective-permute-start(f32[24,384]{1,0:T(8,128)S(1)} %fusion), channel_id=1, source_target_pairs={{0,1},{1,0},{2,3},{3,2},{4,5},{5,4},{6,7},{7,6},{8,9},{9,8},{10,11... | collective-permute-start | bytes 110600 | tf_op jit(solution)/shard_map/ppermute | solution.py:312
